TPU v7x, 128 devices: a whole 4x4x4 slice. The times are simulated.
128 devices in a mesh: ang: 16 (over z_lo, x, core), img: 8 (over z_hi, y).
Axes of the slice: x: 4, y: 4, z: 4 (z_hi: 2, z_lo: 2; z = z_hi * 2 + z_lo), core: 2. Of those that a mesh axis runs over, the one named last changes fastest.
Arguments:
- sinogram: bfloat16 [32, 64, 4096], P('ang', None, 'img'), may hold values from -4 to 28
- offsets: int32 [32], replicated, may hold values from 0 to 65504, as said below
- steps: int32 [32, 2], replicated, may hold values from -32 to 32, as said below
Outputs:
- picture: bfloat16 [1024, 64, 1024], P('ang', None, 'img')
Inputs may be any that keep to these rules, and one draw needn't show every extreme that they name: Each row (u, v) of steps satisfies u^2 + v^2 <= 32^2 < (|u| + 1)^2 + (|v| + 1)^2. For every angle a and every pixel (y, x) with 0 <= x, y < 1024, offsets[a] + steps[a, 0] x + steps[a, 1] y lies in 0 to 65504.
All inputs are finite; a program needn't handle non-finite values.
Results may differ from a plain program's by a relative error of at most 0.0053.
Values may be sent and summed in bfloat16 or wider, within the bound.
A program may use at most 192 MiB of HBM per device.

v0:
```python
import math

import jax
import jax.numpy as jnp
from jax import lax
from jax.sharding import Mesh
from jax.sharding import PartitionSpec as P

BINS = 4096
IMG = 1024
TILE = 32
BAND = 128
IMG_AXES = ("img_0", "img_1")


def in_order(blocks, dim):
    shape = list(blocks.shape[1:])
    shape[dim] *= blocks.shape[0]
    return jnp.moveaxis(blocks, 0, dim).reshape(shape)


def stacked_from(array, axes, sequence):
    blocks = array
    for k in sequence:
        blocks = lax.all_gather(blocks, axes[k])
    done = sequence[::-1]
    back = [done.index(k) for k in range(len(axes))]
    blocks = blocks.transpose(*back, *range(len(axes), blocks.ndim))
    return blocks.reshape(-1, *array.shape)


def gathered_by_axis(array, axes, sequence, dim):
    return in_order(stacked_from(array, axes, sequence), dim)


def ramp_table():
    bin_index = jnp.arange(BINS, dtype=jnp.int32)
    offset_gap = bin_index[None, :] - bin_index[:, None]
    safe_gap = jnp.where(offset_gap == 0, 1, offset_gap).astype(jnp.float32)
    odd_gap = offset_gap % 2 != 0
    kernel = jnp.where(
        offset_gap == 0,
        jnp.float32(0.25),
        jnp.where(odd_gap, -1.0 / (math.pi**2 * safe_gap * safe_gap), jnp.float32(0.0)),
    )
    return kernel


def project_block(filtered, geo_offsets, geo_steps, row_top, row_count, col_left, col_count):
    slices = filtered.shape[1]
    across = col_count // TILE
    block_rows = min(row_count, 8 * TILE)
    while row_count % block_rows:
        block_rows = block_rows - TILE
    tiles_down = block_rows // TILE
    tile_count = tiles_down * across
    tile_order = jnp.arange(tile_count, dtype=jnp.int32)
    tile_top = tile_order // across * TILE
    tile_left = tile_order % across * TILE + col_left
    in_tile = jnp.arange(TILE * TILE, dtype=jnp.int32)
    pix_row = in_tile // TILE
    pix_col = in_tile % TILE
    band_slot = jnp.arange(BAND, dtype=jnp.int32)[None, :, None]

    def one_block(block_no):
        block_top = row_top + block_no * block_rows

        def one_angle(summed, angle_data):
            filtered_one, offset, step_pair = angle_data
            step_x = step_pair[0]
            step_y = step_pair[1]
            corner = offset + step_x * tile_left + step_y * (block_top + tile_top)
            corner = (
                corner + jnp.minimum(step_x, 0) * (TILE - 1) + jnp.minimum(step_y, 0) * (TILE - 1)
            )
            band_start = jnp.minimum(corner // 16, BINS - BAND)
            band_rows = jax.vmap(
                lambda begin_at: lax.dynamic_slice_in_dim(filtered_one, begin_at, BAND, 1)
            )(band_start)
            position = (
                offset
                + step_x * (tile_left[:, None] + pix_col[None, :])
                + step_y * (block_top + tile_top[:, None] + pix_row[None, :])
            )
            low_bin = (position // 16 - band_start[:, None])[:, None, :]
            upper_weight = ((position % 16).astype(jnp.float32) / 16.0)[:, None, :]
            weights = jnp.where(band_slot == low_bin, 1.0 - upper_weight, 0.0) + jnp.where(
                band_slot == low_bin + 1, upper_weight, 0.0
            )
            weights = weights.astype(jnp.bfloat16)
            contrib = jnp.einsum(
                "tsb,tbp->tsp", band_rows, weights, preferred_element_type=jnp.float32
            )
            return (summed + contrib, None)

        start_sum = jnp.zeros((tile_count, slices, TILE * TILE), jnp.float32)
        summed = lax.scan(one_angle, start_sum, (filtered, geo_offsets, geo_steps))[0]
        summed = summed.reshape(tiles_down, across, slices, TILE, TILE)
        return jnp.transpose(summed, (0, 3, 2, 1, 4)).reshape(block_rows, slices, col_count)

    blocks = lax.map(one_block, jnp.arange(row_count // block_rows, dtype=jnp.int32))
    return blocks.reshape(row_count, slices, col_count)


def shards(sinogram, offsets, steps):
    angles_dev = sinogram.shape[0]
    ramp_rows = ramp_table()
    whole_bins = gathered_by_axis(sinogram, IMG_AXES, (0, 1), 2)
    result = jnp.dot(
        whole_bins.reshape(-1, BINS).astype(jnp.float32),
        ramp_rows,
        precision=lax.Precision.HIGHEST,
        preferred_element_type=jnp.float32,
    )
    filtered = result.astype(jnp.bfloat16).reshape(whole_bins.shape[0], whole_bins.shape[1], BINS)
    ang_count = lax.axis_size("ang")
    img_count = lax.axis_size(IMG_AXES)
    rows_dev = IMG // ang_count
    cols_dev = IMG // img_count
    col_left = lax.axis_index(IMG_AXES) * cols_dev
    total_angles = angles_dev * ang_count
    row_first = lax.axis_index("ang") * rows_dev
    partial_value = project_block(
        lax.all_gather(filtered, "ang", axis=0, tiled=True),
        offsets,
        steps,
        row_first,
        rows_dev,
        col_left,
        cols_dev,
    )
    return (partial_value * (2.0 / math.sqrt(total_angles))).astype(jnp.bfloat16)


def solution(mesh):
    finer = Mesh(mesh.devices.reshape(mesh.shape["ang"], 2, 4), ("ang", "img_0", "img_1"))
    return jax.shard_map(
        shards,
        mesh=finer,
        in_specs=(P("ang", None, IMG_AXES), P(), P()),
        out_specs=P("ang", None, IMG_AXES),
        check_vma=False,
    )
```

profile of v0, /device:TPU:1, one launch (start us, length us, event | category | flops | bytes accessed | tf_op | source)
XLA Modules:
  0.0 874.8 jit_solution(12078001420684586321)
XLA Ops:
  6.5 10.1 %all-gather = bf16[4,64,512]{2,1,0:T(8,128)(2,1)} all-gather(bf16[2,64,512]{2,1,0:T(8,128)(2,1)} %param.5), channel_id=2, replica_groups=mesh['ang'=16,'img_0'=2,'img_1'=4] {'img_0'}, dimensions={0}, use_global_device_ids=true | all-gather | bytes 393216 | tf_op jit(solution)/shard_map/all_gather | solution.py:25
  16.7 24.0 %all-gather.7.cloned.1.call-done = bf16[8,2,64,512]{3,2,1,0:T(8,128)(2,1)} async-done(((bf16[2,2,64,512]{3,2,1,0:T(8,128)(2,1)}), bf16[8,2,64,512]{3,2,1,0:T(8,128)(2,1)}) %all-gather.7.cloned.1.call-update) | async-done | bytes 1048592 | tf_op jit(solution)/shard_map/all_gather | solution.py:25
  43.1 76.2 %fusion.51 = bf16[4096,128]{0,1:T(8,128)(2,1)} fusion(bf16[128,4096]{1,0:T(8,128)(2,1)S(1)} %bitcast.59), kind=kOutput, calls=%fused_computation.89 | convolution fusion | flops 26122649600 | bytes 2097152 | tf_op jit(solution)/shard_map/dot_general | solution.py:109
  119.3 93.4 %all-gather.5.cloned.1.call-done = bf16[32,64,4096]{2,1,0:T(8,128)(2,1)} async-done(((bf16[2,64,4096]{2,1,0:T(8,128)(2,1)}), bf16[32,64,4096]{2,1,0:T(8,128)(2,1)}) %all-gather.5.cloned.1.call-update) | async-done | bytes 16777232 | tf_op jit(solution)/shard_map/all_gather | solution.py:124
  212.7 647.6 %while.27 = (s32[]{:T(128)}, f32[8,64,1024]{2,1,0:T(8,128)S(1)}, bf16[32,64,4096]{2,1,0:T(8,128)(2,1)}, s32[32]{0:T(128)S(1)}, s32[32,2]{0,1:T(2,128)S(1)}, /*in...) while((s32[]{:T(128)}, f32[8,64,1024]{2,1,0:T(8,128)S(1)}, ...), condition=%wide.region_1.2_spmd.clone.clone, body=%wide.region_0.1_spmd.clone.clone.sunk | while | flops 141922896 | bytes 5694332 | solution.py:97
  216.9 1.9 fusion.71
  221.8 9.7 %while.28 = (s32[]{:T(128)}, bf16[64,4096]{1,0:T(8,128)(2,1)S(1)}, s32[8,2]{0,1:T(2,128)S(1)}, bf16[8,64,128]{2,1,0:T(8,128)(2,1)S(1)}, s32[]{:T(128)}) while((s32[]{:T(128)}, bf16[64,4096]{1,0:T(8,128)(2,1)S(1)}, s32[8,2]{0,1:T(2,128)S(1)}, bf16[8,64,128]{2,1,0:T(8,128)(2,1)S(1)}, s32[]{:T(128)}) %tuple.73), condition=%wide.while_cond, body=%wide.while_body.sunk | while | flops 2 | bytes 32873 | solution.py:78
  237.2 1.9 fusion.71
  242.1 9.7 %while.28 = (s32[]{:T(128)}, bf16[64,4096]{1,0:T(8,128)(2,1)S(1)}, s32[8,2]{0,1:T(2,128)S(1)}, bf16[8,64,128]{2,1,0:T(8,128)(2,1)S(1)}, s32[]{:T(128)}) while((s32[]{:T(128)}, bf16[64,4096]{1,0:T(8,128)(2,1)S(1)}, s32[8,2]{0,1:T(2,128)S(1)}, bf16[8,64,128]{2,1,0:T(8,128)(2,1)S(1)}, s32[]{:T(128)}) %tuple.73), condition=%wide.while_cond, body=%wide.while_body.sunk | while | flops 2 | bytes 32873 | solution.py:78
  257.4 1.9 fusion.71
  262.3 9.7 %while.28 = (s32[]{:T(128)}, bf16[64,4096]{1,0:T(8,128)(2,1)S(1)}, s32[8,2]{0,1:T(2,128)S(1)}, bf16[8,64,128]{2,1,0:T(8,128)(2,1)S(1)}, s32[]{:T(128)}) while((s32[]{:T(128)}, bf16[64,4096]{1,0:T(8,128)(2,1)S(1)}, s32[8,2]{0,1:T(2,128)S(1)}, bf16[8,64,128]{2,1,0:T(8,128)(2,1)S(1)}, s32[]{:T(128)}) %tuple.73), condition=%wide.while_cond, body=%wide.while_body.sunk | while | flops 2 | bytes 32873 | solution.py:78
  277.7 1.9 fusion.71
  282.5 9.7 %while.28 = (s32[]{:T(128)}, bf16[64,4096]{1,0:T(8,128)(2,1)S(1)}, s32[8,2]{0,1:T(2,128)S(1)}, bf16[8,64,128]{2,1,0:T(8,128)(2,1)S(1)}, s32[]{:T(128)}) while((s32[]{:T(128)}, bf16[64,4096]{1,0:T(8,128)(2,1)S(1)}, s32[8,2]{0,1:T(2,128)S(1)}, bf16[8,64,128]{2,1,0:T(8,128)(2,1)S(1)}, s32[]{:T(128)}) %tuple.73), condition=%wide.while_cond, body=%wide.while_body.sunk | while | flops 2 | bytes 32873 | solution.py:78
  297.9 1.9 fusion.71
  302.8 9.7 %while.28 = (s32[]{:T(128)}, bf16[64,4096]{1,0:T(8,128)(2,1)S(1)}, s32[8,2]{0,1:T(2,128)S(1)}, bf16[8,64,128]{2,1,0:T(8,128)(2,1)S(1)}, s32[]{:T(128)}) while((s32[]{:T(128)}, bf16[64,4096]{1,0:T(8,128)(2,1)S(1)}, s32[8,2]{0,1:T(2,128)S(1)}, bf16[8,64,128]{2,1,0:T(8,128)(2,1)S(1)}, s32[]{:T(128)}) %tuple.73), condition=%wide.while_cond, body=%wide.while_body.sunk | while | flops 2 | bytes 32873 | solution.py:78
  318.1 1.9 fusion.71
  323.0 9.7 %while.28 = (s32[]{:T(128)}, bf16[64,4096]{1,0:T(8,128)(2,1)S(1)}, s32[8,2]{0,1:T(2,128)S(1)}, bf16[8,64,128]{2,1,0:T(8,128)(2,1)S(1)}, s32[]{:T(128)}) while((s32[]{:T(128)}, bf16[64,4096]{1,0:T(8,128)(2,1)S(1)}, s32[8,2]{0,1:T(2,128)S(1)}, bf16[8,64,128]{2,1,0:T(8,128)(2,1)S(1)}, s32[]{:T(128)}) %tuple.73), condition=%wide.while_cond, body=%wide.while_body.sunk | while | flops 2 | bytes 32873 | solution.py:78
  338.4 1.9 fusion.71
  343.2 9.7 %while.28 = (s32[]{:T(128)}, bf16[64,4096]{1,0:T(8,128)(2,1)S(1)}, s32[8,2]{0,1:T(2,128)S(1)}, bf16[8,64,128]{2,1,0:T(8,128)(2,1)S(1)}, s32[]{:T(128)}) while((s32[]{:T(128)}, bf16[64,4096]{1,0:T(8,128)(2,1)S(1)}, s32[8,2]{0,1:T(2,128)S(1)}, bf16[8,64,128]{2,1,0:T(8,128)(2,1)S(1)}, s32[]{:T(128)}) %tuple.73), condition=%wide.while_cond, body=%wide.while_body.sunk | while | flops 2 | bytes 32873 | solution.py:78
  358.6 1.9 fusion.71
  363.5 9.7 %while.28 = (s32[]{:T(128)}, bf16[64,4096]{1,0:T(8,128)(2,1)S(1)}, s32[8,2]{0,1:T(2,128)S(1)}, bf16[8,64,128]{2,1,0:T(8,128)(2,1)S(1)}, s32[]{:T(128)}) while((s32[]{:T(128)}, bf16[64,4096]{1,0:T(8,128)(2,1)S(1)}, s32[8,2]{0,1:T(2,128)S(1)}, bf16[8,64,128]{2,1,0:T(8,128)(2,1)S(1)}, s32[]{:T(128)}) %tuple.73), condition=%wide.while_cond, body=%wide.while_body.sunk | while | flops 2 | bytes 32873 | solution.py:78
  378.8 1.9 fusion.71
  383.7 9.7 %while.28 = (s32[]{:T(128)}, bf16[64,4096]{1,0:T(8,128)(2,1)S(1)}, s32[8,2]{0,1:T(2,128)S(1)}, bf16[8,64,128]{2,1,0:T(8,128)(2,1)S(1)}, s32[]{:T(128)}) while((s32[]{:T(128)}, bf16[64,4096]{1,0:T(8,128)(2,1)S(1)}, s32[8,2]{0,1:T(2,128)S(1)}, bf16[8,64,128]{2,1,0:T(8,128)(2,1)S(1)}, s32[]{:T(128)}) %tuple.73), condition=%wide.while_cond, body=%wide.while_body.sunk | while | flops 2 | bytes 32873 | solution.py:78
  399.1 1.9 fusion.71
  404.0 9.7 %while.28 = (s32[]{:T(128)}, bf16[64,4096]{1,0:T(8,128)(2,1)S(1)}, s32[8,2]{0,1:T(2,128)S(1)}, bf16[8,64,128]{2,1,0:T(8,128)(2,1)S(1)}, s32[]{:T(128)}) while((s32[]{:T(128)}, bf16[64,4096]{1,0:T(8,128)(2,1)S(1)}, s32[8,2]{0,1:T(2,128)S(1)}, bf16[8,64,128]{2,1,0:T(8,128)(2,1)S(1)}, s32[]{:T(128)}) %tuple.73), condition=%wide.while_cond, body=%wide.while_body.sunk | while | flops 2 | bytes 32873 | solution.py:78
  419.3 1.9 fusion.71
  424.2 9.7 %while.28 = (s32[]{:T(128)}, bf16[64,4096]{1,0:T(8,128)(2,1)S(1)}, s32[8,2]{0,1:T(2,128)S(1)}, bf16[8,64,128]{2,1,0:T(8,128)(2,1)S(1)}, s32[]{:T(128)}) while((s32[]{:T(128)}, bf16[64,4096]{1,0:T(8,128)(2,1)S(1)}, s32[8,2]{0,1:T(2,128)S(1)}, bf16[8,64,128]{2,1,0:T(8,128)(2,1)S(1)}, s32[]{:T(128)}) %tuple.73), condition=%wide.while_cond, body=%wide.while_body.sunk | while | flops 2 | bytes 32873 | solution.py:78
  439.6 1.9 fusion.71
  444.4 9.7 %while.28 = (s32[]{:T(128)}, bf16[64,4096]{1,0:T(8,128)(2,1)S(1)}, s32[8,2]{0,1:T(2,128)S(1)}, bf16[8,64,128]{2,1,0:T(8,128)(2,1)S(1)}, s32[]{:T(128)}) while((s32[]{:T(128)}, bf16[64,4096]{1,0:T(8,128)(2,1)S(1)}, s32[8,2]{0,1:T(2,128)S(1)}, bf16[8,64,128]{2,1,0:T(8,128)(2,1)S(1)}, s32[]{:T(128)}) %tuple.73), condition=%wide.while_cond, body=%wide.while_body.sunk | while | flops 2 | bytes 32873 | solution.py:78
  459.8 1.9 fusion.71
  464.7 9.7 %while.28 = (s32[]{:T(128)}, bf16[64,4096]{1,0:T(8,128)(2,1)S(1)}, s32[8,2]{0,1:T(2,128)S(1)}, bf16[8,64,128]{2,1,0:T(8,128)(2,1)S(1)}, s32[]{:T(128)}) while((s32[]{:T(128)}, bf16[64,4096]{1,0:T(8,128)(2,1)S(1)}, s32[8,2]{0,1:T(2,128)S(1)}, bf16[8,64,128]{2,1,0:T(8,128)(2,1)S(1)}, s32[]{:T(128)}) %tuple.73), condition=%wide.while_cond, body=%wide.while_body.sunk | while | flops 2 | bytes 32873 | solution.py:78
  480.0 1.9 fusion.71
  484.9 9.7 %while.28 = (s32[]{:T(128)}, bf16[64,4096]{1,0:T(8,128)(2,1)S(1)}, s32[8,2]{0,1:T(2,128)S(1)}, bf16[8,64,128]{2,1,0:T(8,128)(2,1)S(1)}, s32[]{:T(128)}) while((s32[]{:T(128)}, bf16[64,4096]{1,0:T(8,128)(2,1)S(1)}, s32[8,2]{0,1:T(2,128)S(1)}, bf16[8,64,128]{2,1,0:T(8,128)(2,1)S(1)}, s32[]{:T(128)}) %tuple.73), condition=%wide.while_cond, body=%wide.while_body.sunk | while | flops 2 | bytes 32873 | solution.py:78
  500.3 1.9 fusion.71
  505.1 9.7 %while.28 = (s32[]{:T(128)}, bf16[64,4096]{1,0:T(8,128)(2,1)S(1)}, s32[8,2]{0,1:T(2,128)S(1)}, bf16[8,64,128]{2,1,0:T(8,128)(2,1)S(1)}, s32[]{:T(128)}) while((s32[]{:T(128)}, bf16[64,4096]{1,0:T(8,128)(2,1)S(1)}, s32[8,2]{0,1:T(2,128)S(1)}, bf16[8,64,128]{2,1,0:T(8,128)(2,1)S(1)}, s32[]{:T(128)}) %tuple.73), condition=%wide.while_cond, body=%wide.while_body.sunk | while | flops 2 | bytes 32873 | solution.py:78
  520.5 1.9 fusion.71
  525.4 9.7 %while.28 = (s32[]{:T(128)}, bf16[64,4096]{1,0:T(8,128)(2,1)S(1)}, s32[8,2]{0,1:T(2,128)S(1)}, bf16[8,64,128]{2,1,0:T(8,128)(2,1)S(1)}, s32[]{:T(128)}) while((s32[]{:T(128)}, bf16[64,4096]{1,0:T(8,128)(2,1)S(1)}, s32[8,2]{0,1:T(2,128)S(1)}, bf16[8,64,128]{2,1,0:T(8,128)(2,1)S(1)}, s32[]{:T(128)}) %tuple.73), condition=%wide.while_cond, body=%wide.while_body.sunk | while | flops 2 | bytes 32873 | solution.py:78
  540.7 1.9 fusion.71
  545.6 9.7 %while.28 = (s32[]{:T(128)}, bf16[64,4096]{1,0:T(8,128)(2,1)S(1)}, s32[8,2]{0,1:T(2,128)S(1)}, bf16[8,64,128]{2,1,0:T(8,128)(2,1)S(1)}, s32[]{:T(128)}) while((s32[]{:T(128)}, bf16[64,4096]{1,0:T(8,128)(2,1)S(1)}, s32[8,2]{0,1:T(2,128)S(1)}, bf16[8,64,128]{2,1,0:T(8,128)(2,1)S(1)}, s32[]{:T(128)}) %tuple.73), condition=%wide.while_cond, body=%wide.while_body.sunk | while | flops 2 | bytes 32873 | solution.py:78
  561.0 1.9 fusion.71
  565.9 9.7 %while.28 = (s32[]{:T(128)}, bf16[64,4096]{1,0:T(8,128)(2,1)S(1)}, s32[8,2]{0,1:T(2,128)S(1)}, bf16[8,64,128]{2,1,0:T(8,128)(2,1)S(1)}, s32[]{:T(128)}) while((s32[]{:T(128)}, bf16[64,4096]{1,0:T(8,128)(2,1)S(1)}, s32[8,2]{0,1:T(2,128)S(1)}, bf16[8,64,128]{2,1,0:T(8,128)(2,1)S(1)}, s32[]{:T(128)}) %tuple.73), condition=%wide.while_cond, body=%wide.while_body.sunk | while | flops 2 | bytes 32873 | solution.py:78
  581.2 1.9 fusion.71
  586.1 9.7 %while.28 = (s32[]{:T(128)}, bf16[64,4096]{1,0:T(8,128)(2,1)S(1)}, s32[8,2]{0,1:T(2,128)S(1)}, bf16[8,64,128]{2,1,0:T(8,128)(2,1)S(1)}, s32[]{:T(128)}) while((s32[]{:T(128)}, bf16[64,4096]{1,0:T(8,128)(2,1)S(1)}, s32[8,2]{0,1:T(2,128)S(1)}, bf16[8,64,128]{2,1,0:T(8,128)(2,1)S(1)}, s32[]{:T(128)}) %tuple.73), condition=%wide.while_cond, body=%wide.while_body.sunk | while | flops 2 | bytes 32873 | solution.py:78
  601.5 1.9 fusion.71
  606.3 9.7 %while.28 = (s32[]{:T(128)}, bf16[64,4096]{1,0:T(8,128)(2,1)S(1)}, s32[8,2]{0,1:T(2,128)S(1)}, bf16[8,64,128]{2,1,0:T(8,128)(2,1)S(1)}, s32[]{:T(128)}) while((s32[]{:T(128)}, bf16[64,4096]{1,0:T(8,128)(2,1)S(1)}, s32[8,2]{0,1:T(2,128)S(1)}, bf16[8,64,128]{2,1,0:T(8,128)(2,1)S(1)}, s32[]{:T(128)}) %tuple.73), condition=%wide.while_cond, body=%wide.while_body.sunk | while | flops 2 | bytes 32873 | solution.py:78
  621.7 1.9 fusion.71
  626.6 9.7 %while.28 = (s32[]{:T(128)}, bf16[64,4096]{1,0:T(8,128)(2,1)S(1)}, s32[8,2]{0,1:T(2,128)S(1)}, bf16[8,64,128]{2,1,0:T(8,128)(2,1)S(1)}, s32[]{:T(128)}) while((s32[]{:T(128)}, bf16[64,4096]{1,0:T(8,128)(2,1)S(1)}, s32[8,2]{0,1:T(2,128)S(1)}, bf16[8,64,128]{2,1,0:T(8,128)(2,1)S(1)}, s32[]{:T(128)}) %tuple.73), condition=%wide.while_cond, body=%wide.while_body.sunk | while | flops 2 | bytes 32873 | solution.py:78
  641.9 1.9 fusion.71
  646.8 9.7 %while.28 = (s32[]{:T(128)}, bf16[64,4096]{1,0:T(8,128)(2,1)S(1)}, s32[8,2]{0,1:T(2,128)S(1)}, bf16[8,64,128]{2,1,0:T(8,128)(2,1)S(1)}, s32[]{:T(128)}) while((s32[]{:T(128)}, bf16[64,4096]{1,0:T(8,128)(2,1)S(1)}, s32[8,2]{0,1:T(2,128)S(1)}, bf16[8,64,128]{2,1,0:T(8,128)(2,1)S(1)}, s32[]{:T(128)}) %tuple.73), condition=%wide.while_cond, body=%wide.while_body.sunk | while | flops 2 | bytes 32873 | solution.py:78
  662.2 1.9 fusion.71
  667.0 9.7 %while.28 = (s32[]{:T(128)}, bf16[64,4096]{1,0:T(8,128)(2,1)S(1)}, s32[8,2]{0,1:T(2,128)S(1)}, bf16[8,64,128]{2,1,0:T(8,128)(2,1)S(1)}, s32[]{:T(128)}) while((s32[]{:T(128)}, bf16[64,4096]{1,0:T(8,128)(2,1)S(1)}, s32[8,2]{0,1:T(2,128)S(1)}, bf16[8,64,128]{2,1,0:T(8,128)(2,1)S(1)}, s32[]{:T(128)}) %tuple.73), condition=%wide.while_cond, body=%wide.while_body.sunk | while | flops 2 | bytes 32873 | solution.py:78
  687.3 9.7 %while.28 = (s32[]{:T(128)}, bf16[64,4096]{1,0:T(8,128)(2,1)S(1)}, s32[8,2]{0,1:T(2,128)S(1)}, bf16[8,64,128]{2,1,0:T(8,128)(2,1)S(1)}, s32[]{:T(128)}) while((s32[]{:T(128)}, bf16[64,4096]{1,0:T(8,128)(2,1)S(1)}, s32[8,2]{0,1:T(2,128)S(1)}, bf16[8,64,128]{2,1,0:T(8,128)(2,1)S(1)}, s32[]{:T(128)}) %tuple.73), condition=%wide.while_cond, body=%wide.while_body.sunk | while | flops 2 | bytes 32873 | solution.py:78
  707.5 9.7 %while.28 = (s32[]{:T(128)}, bf16[64,4096]{1,0:T(8,128)(2,1)S(1)}, s32[8,2]{0,1:T(2,128)S(1)}, bf16[8,64,128]{2,1,0:T(8,128)(2,1)S(1)}, s32[]{:T(128)}) while((s32[]{:T(128)}, bf16[64,4096]{1,0:T(8,128)(2,1)S(1)}, s32[8,2]{0,1:T(2,128)S(1)}, bf16[8,64,128]{2,1,0:T(8,128)(2,1)S(1)}, s32[]{:T(128)}) %tuple.73), condition=%wide.while_cond, body=%wide.while_body.sunk | while | flops 2 | bytes 32873 | solution.py:78
  727.8 9.7 %while.28 = (s32[]{:T(128)}, bf16[64,4096]{1,0:T(8,128)(2,1)S(1)}, s32[8,2]{0,1:T(2,128)S(1)}, bf16[8,64,128]{2,1,0:T(8,128)(2,1)S(1)}, s32[]{:T(128)}) while((s32[]{:T(128)}, bf16[64,4096]{1,0:T(8,128)(2,1)S(1)}, s32[8,2]{0,1:T(2,128)S(1)}, bf16[8,64,128]{2,1,0:T(8,128)(2,1)S(1)}, s32[]{:T(128)}) %tuple.73), condition=%wide.while_cond, body=%wide.while_body.sunk | while | flops 2 | bytes 32873 | solution.py:78
  748.0 9.7 %while.28 = (s32[]{:T(128)}, bf16[64,4096]{1,0:T(8,128)(2,1)S(1)}, s32[8,2]{0,1:T(2,128)S(1)}, bf16[8,64,128]{2,1,0:T(8,128)(2,1)S(1)}, s32[]{:T(128)}) while((s32[]{:T(128)}, bf16[64,4096]{1,0:T(8,128)(2,1)S(1)}, s32[8,2]{0,1:T(2,128)S(1)}, bf16[8,64,128]{2,1,0:T(8,128)(2,1)S(1)}, s32[]{:T(128)}) %tuple.73), condition=%wide.while_cond, body=%wide.while_body.sunk | while | flops 2 | bytes 32873 | solution.py:78
  768.2 9.7 %while.28 = (s32[]{:T(128)}, bf16[64,4096]{1,0:T(8,128)(2,1)S(1)}, s32[8,2]{0,1:T(2,128)S(1)}, bf16[8,64,128]{2,1,0:T(8,128)(2,1)S(1)}, s32[]{:T(128)}) while((s32[]{:T(128)}, bf16[64,4096]{1,0:T(8,128)(2,1)S(1)}, s32[8,2]{0,1:T(2,128)S(1)}, bf16[8,64,128]{2,1,0:T(8,128)(2,1)S(1)}, s32[]{:T(128)}) %tuple.73), condition=%wide.while_cond, body=%wide.while_body.sunk | while | flops 2 | bytes 32873 | solution.py:78
  783.6 1.9 fusion.71
  788.5 9.7 %while.28 = (s32[]{:T(128)}, bf16[64,4096]{1,0:T(8,128)(2,1)S(1)}, s32[8,2]{0,1:T(2,128)S(1)}, bf16[8,64,128]{2,1,0:T(8,128)(2,1)S(1)}, s32[]{:T(128)}) while((s32[]{:T(128)}, bf16[64,4096]{1,0:T(8,128)(2,1)S(1)}, s32[8,2]{0,1:T(2,128)S(1)}, bf16[8,64,128]{2,1,0:T(8,128)(2,1)S(1)}, s32[]{:T(128)}) %tuple.73), condition=%wide.while_cond, body=%wide.while_body.sunk | while | flops 2 | bytes 32873 | solution.py:78
  808.7 9.7 %while.28 = (s32[]{:T(128)}, bf16[64,4096]{1,0:T(8,128)(2,1)S(1)}, s32[8,2]{0,1:T(2,128)S(1)}, bf16[8,64,128]{2,1,0:T(8,128)(2,1)S(1)}, s32[]{:T(128)}) while((s32[]{:T(128)}, bf16[64,4096]{1,0:T(8,128)(2,1)S(1)}, s32[8,2]{0,1:T(2,128)S(1)}, bf16[8,64,128]{2,1,0:T(8,128)(2,1)S(1)}, s32[]{:T(128)}) %tuple.73), condition=%wide.while_cond, body=%wide.while_body.sunk | while | flops 2 | bytes 32873 | solution.py:78
  824.1 1.9 fusion.71
  828.9 9.7 %while.28 = (s32[]{:T(128)}, bf16[64,4096]{1,0:T(8,128)(2,1)S(1)}, s32[8,2]{0,1:T(2,128)S(1)}, bf16[8,64,128]{2,1,0:T(8,128)(2,1)S(1)}, s32[]{:T(128)}) while((s32[]{:T(128)}, bf16[64,4096]{1,0:T(8,128)(2,1)S(1)}, s32[8,2]{0,1:T(2,128)S(1)}, bf16[8,64,128]{2,1,0:T(8,128)(2,1)S(1)}, s32[]{:T(128)}) %tuple.73), condition=%wide.while_cond, body=%wide.while_body.sunk | while | flops 2 | bytes 32873 | solution.py:78
  849.2 9.7 %while.28 = (s32[]{:T(128)}, bf16[64,4096]{1,0:T(8,128)(2,1)S(1)}, s32[8,2]{0,1:T(2,128)S(1)}, bf16[8,64,128]{2,1,0:T(8,128)(2,1)S(1)}, s32[]{:T(128)}) while((s32[]{:T(128)}, bf16[64,4096]{1,0:T(8,128)(2,1)S(1)}, s32[8,2]{0,1:T(2,128)S(1)}, bf16[8,64,128]{2,1,0:T(8,128)(2,1)S(1)}, s32[]{:T(128)}) %tuple.73), condition=%wide.while_cond, body=%wide.while_body.sunk | while | flops 2 | bytes 32873 | solution.py:78
  860.3 2.7 copy.16
  863.0 2.6 multiply_convert_fusion
  (1173 shorter events, 562.7 us)
Async XLA Ops:
  6.5 34.2 %all-gather.7.cloned.1.call-start = ((), (), s32[]{:S(2)}) async-start(), calls=%async_computation.1 | async-start | bytes 1310720 | tf_op jit(solution)/shard_map/all_gather | solution.py:25
  16.7 196.0 %all-gather.5.cloned.1.call-start = ((), (), s32[]{:S(2)}) async-start(), calls=%async_computation | async-start | bytes 17825792 | tf_op jit(solution)/shard_map/all_gather | solution.py:124
  43.0 169.7 %copy-start = (s32[32,2]{0,1:T(2,128)S(1)}, s32[32,2]{0,1:T(2,128)}, u32[]{:S(2)}) copy-start(s32[32,2]{0,1:T(2,128)} %param.7) | copy-start | bytes 772
  43.1 169.6 %copy-start.1 = (s32[32]{0:T(128)S(1)}, s32[32]{0:T(128)}, u32[]{:S(2)}) copy-start(s32[32]{0:T(128)} %param.6) | copy-start | bytes 388
Sparse Core Ops, SparseCore 0:
  16.8 23.9 all-gather.6
  119.4 93.2 all-gather.4
where the time goes:
time: 881 us; the launch traced here: 875 us
  local copies, waits for them, and re-layouts  390 us (44%)
  other arithmetic  182 us (21%)
  matrix products  120 us (14%)
  waiting for transfers between devices  117 us (13%)
  loops' own time  42.2 us (5%)
  between operations  13.5 us (2%)
  blocking collectives  10.1 us (1%)
    gather x768, local copies, waits for them, and re-layouts  307 us
    all_gather x1, waiting for transfers between devices, shards(): lax.all_gather(filtered, 'ang', axis=0, tiled=True)  93.4 us
    dot_general x1, matrix products, shards(): jnp.dot(whole_bins.reshape(-1, BINS).astype(jnp.float32), ramp_rows, prec...  76.2 us
    sub x32, other arithmetic, one_angle(): low_bin = (position // 16 - band_start[:, None])[:, None, :]  60.5 us
    sub x32, other arithmetic, one_angle(): 1.0 - upper_weight  60.4 us
    min x32, other arithmetic, one_angle(): band_start = jnp.minimum(corner // 16, BINS - BAND)  57.9 us
    dot_general x32, matrix products, one_angle(): jnp.einsum('tsb,tbp->tsp', band_rows, weights, preferred_element_type=jnp...  43.4 us
    another operation x1, loops' own time, one_block(): lax.scan(one_angle, start_sum, (filtered, geo_offsets, geo_steps))[0]  38.2 us
  transfers between devices with their start and end apart: 2, of which 2 were waited for; matrix products, arithmetic and copies ran while one was open for 0% of the time, Pallas kernels for 0%

commit v1 on v0

v1 whole, which is shorter than its diff:
```python
import math

import jax
import jax.numpy as jnp
from jax import lax
from jax.experimental import pallas as pl
from jax.experimental.pallas import tpu as pltpu
from jax.sharding import PartitionSpec as P

BINS = 4096
IMG = 1024
ANGLES = 32
SLICES = 64
ANG = 16
IMGD = 8
CHIPS = 64
ROWS = IMG // ANG
COLS = IMG // IMGD
TILE = 32
GROUP = 16
MESH = pl.DeviceIdType.MESH
VMEM = pl.BlockSpec(memory_space=pltpu.VMEM)
SMEM = pl.BlockSpec(memory_space=pltpu.SMEM)
LIMIT = 48 * 1024 * 1024


def exchange_rows(sino, recv, local_sem, send_sem, recv_sem):
    i = lax.axis_index("ang")
    j = lax.axis_index("img")
    barrier = pltpu.get_barrier_semaphore()
    for k in range(1, IMGD):
        pl.semaphore_signal(barrier, inc=1, device_id=(i, lax.rem(j + k, IMGD)), device_id_type=MESH)
    own = pltpu.make_async_copy(sino.at[j], recv.at[j], local_sem)
    own.start()
    pl.semaphore_wait(barrier, IMGD - 1)

    def copy(k):
        to = lax.rem(j + k, IMGD)
        return pltpu.make_async_remote_copy(
            src_ref=sino.at[to],
            dst_ref=recv.at[j],
            send_sem=send_sem.at[k],
            recv_sem=recv_sem.at[k],
            device_id=(i, to),
            device_id_type=MESH,
        )

    copies = [copy(k) for k in range(1, IMGD)]
    for c in copies:
        c.start()
    own.wait()
    for c in copies:
        c.wait()


def ramp_tiles(ramp_hi, ramp_fine):
    gap = lax.broadcasted_iota(jnp.int32, (128, 128), 1) - lax.broadcasted_iota(jnp.int32, (128, 128), 0)
    scale = jnp.where((gap & 1) != 0, jnp.float32(-1.0 / math.pi**2), jnp.float32(0.0))
    gap_f = gap.astype(jnp.float32)

    def value(e):
        t = gap_f + jnp.asarray(128 * e).astype(jnp.float32)
        t = jnp.where(t == 0.0, jnp.float32(1.0), t)
        return scale / (t * t)

    @pl.loop(0, 64)
    def _(e):
        ramp_hi[e] = value(e - 32).astype(jnp.bfloat16)

    for e in range(-3, 4):
        v = value(e)
        if e == 0:
            v = jnp.where(gap == 0, jnp.float32(0.25), v)
        hi = v.astype(jnp.bfloat16)
        rest = v - hi.astype(jnp.float32)
        mid = rest.astype(jnp.bfloat16)
        low = (rest - mid.astype(jnp.float32)).astype(jnp.bfloat16)
        ramp_hi[e + 32] = hi
        ramp_fine[0, e + 3] = mid
        ramp_fine[1, e + 3] = low


def toeplitz(tiles, at):
    top = jnp.concatenate([tiles[at], tiles[at + 1]], axis=1)
    low = jnp.concatenate([tiles[at - 1], tiles[at]], axis=1)
    return jnp.concatenate([top, low], axis=0)


def filter_rows(x, acc, ramp_hi, ramp_fine):
    acc[...] = jnp.zeros_like(acc)
    for d in sorted(range(-15, 16), key=abs):
        count = 16 - abs(d)
        lhs = x[pl.ds(max(0, -d), count)].reshape(count * GROUP, 256)
        total = jnp.dot(lhs, toeplitz(ramp_hi, 2 * d + 32), preferred_element_type=jnp.float32)
        if abs(d) <= 1:
            for term in range(2):
                total += jnp.dot(
                    lhs, toeplitz(ramp_fine.at[term], 2 * d + 3), preferred_element_type=jnp.float32
                )
        acc[pl.ds(max(0, d), count)] += total.reshape(count, GROUP, 256)


def angle_data(offsets, steps, a):
    u = steps[a, 0]
    v = steps[a, 1]
    return offsets[a], u, v, jnp.minimum(u, 0) + jnp.minimum(v, 0)


def window_start(offset, u, v, low, chip_row, img):
    return (offset + u * (COLS * img) + v * (2 * ROWS * chip_row) + low * 127) >> 4


def pack_windows(filt, packed, offsets, steps):
    i = lax.axis_index("ang")
    j = lax.axis_index("img")
    offset, u, v, low = angle_data(offsets, steps, 2 * i + j // 4)
    lane = lax.broadcasted_iota(jnp.int32, (GROUP, 128), 1)

    @pl.loop(0, CHIPS)
    def _(d):
        ws = window_start(offset, u, v, low, d // IMGD, d % IMGD)
        shift = ws & 127
        blocks = filt[pl.ds(ws >> 7, 4)]
        back = (128 - shift) & 127
        rolled = [pltpu.roll(blocks[k], back, 1) for k in range(4)]
        for k in range(3):
            packed[d, k] = jnp.where(lane < 128 - shift, rolled[k], rolled[k + 1]).astype(jnp.bfloat16)


def filter_kernel(offsets, steps, recv, packed, ramp_hi, ramp_fine, x, acc, filt):
    ramp_tiles(ramp_hi, ramp_fine)
    for b in range(16):
        x[b] = recv[b // 2, :, pl.ds(256 * (b % 2), 256)]
    filter_rows(x, acc, ramp_hi, ramp_fine)
    for b in range(16):
        for h in range(2):
            filt[2 * b + h] = acc[b, :, pl.ds(128 * h, 128)]
    filt[pl.ds(32, 4)] = jnp.zeros((4, GROUP, 128), jnp.float32)
    pack_windows(filt, packed, offsets, steps)


def exchange_windows(packed, recv, local_sem, send_sem, recv_sem, sib_send, sib_recv):
    i = lax.axis_index("ang")
    j = lax.axis_index("img")
    core = lax.rem(i, 2)
    row = i // 2
    me = row * IMGD + j
    barrier = pltpu.get_barrier_semaphore()

    @pl.loop(1, CHIPS)
    def _(k):
        to = lax.rem(me + k, CHIPS)
        pl.semaphore_signal(
            barrier, inc=1, device_id=(2 * (to // IMGD) + core, lax.rem(to, IMGD)), device_id_type=MESH
        )

    sibling = (2 * row + 1 - core, j)
    pl.semaphore_signal(barrier, inc=1, device_id=sibling, device_id_type=MESH)
    own = pltpu.make_async_copy(packed.at[me], recv.at[core, row, j], local_sem)
    own.start()
    pl.semaphore_wait(barrier, CHIPS)

    def copy(k):
        to = lax.rem(me + k, CHIPS)
        return pltpu.make_async_remote_copy(
            src_ref=packed.at[to],
            dst_ref=recv.at[core, row, j],
            send_sem=send_sem.at[k],
            recv_sem=recv_sem.at[k],
            device_id=(2 * (to // IMGD) + core, lax.rem(to, IMGD)),
            device_id_type=MESH,
        )

    @pl.loop(1, CHIPS)
    def _(k):
        copy(k).start()

    own.wait()

    @pl.loop(1, CHIPS)
    def _(k):
        copy(k).wait()

    share = pltpu.make_async_remote_copy(
        src_ref=recv.at[core],
        dst_ref=recv.at[core],
        send_sem=sib_send,
        recv_sem=sib_recv,
        device_id=sibling,
        device_id_type=MESH,
    )
    share.start()
    share.wait()


def project_kernel(offsets, steps, recv, out, lhs, weights, acc):
    i = lax.axis_index("ang")
    j = lax.axis_index("img")
    lane = lax.broadcasted_iota(jnp.int32, (1, 128), 1)
    pixel = lax.broadcasted_iota(jnp.int32, (1, TILE * TILE), 1)
    px = (pixel & (TILE - 1)).astype(jnp.float32)
    py = (pixel >> 5).astype(jnp.float32)
    slot = lax.broadcasted_iota(jnp.int32, (128, TILE * TILE), 0).astype(jnp.float32)
    acc[...] = jnp.zeros_like(acc)

    @pl.loop(0, ANGLES // 2)
    def _(pair):
        source = (pair % 8) * 4 + (pair // 8) * 2
        for a in range(2):
            offset, u, v, low = angle_data(offsets, steps, source + a)
            first = ((offset + low * (TILE - 1)) & 15) - low * (TILE - 1)
            where = (first.astype(jnp.float32) + u.astype(jnp.float32) * px + v.astype(jnp.float32) * py) * 0.0625
            weights[pl.ds(128 * a, 128)] = jnp.maximum(1.0 - jnp.abs(slot - where), 0.0).astype(jnp.bfloat16)
            ws = window_start(offset, u, v, low, i // 2, j)
            for tile in range(8):
                ty, tx = tile // 4, tile % 4
                corner = offset + u * (COLS * j + TILE * tx) + v * (ROWS * i + TILE * ty) + low * (TILE - 1)
                begin = (corner >> 4) - ws
                block = begin >> 7
                shift = begin & 127
                back = (128 - shift) & 127
                after = jnp.minimum(block + 1, 2)
                for g in range(4):
                    left = recv[2 * pair + a, g, block].astype(jnp.float32)
                    right = recv[2 * pair + a, g, after].astype(jnp.float32)
                    left = pltpu.roll(left, back, 1)
                    right = pltpu.roll(right, back, 1)
                    band = jnp.where(lane < 128 - shift, left, right).astype(jnp.bfloat16)
                    lhs[pl.ds(tile * SLICES + g * GROUP, GROUP), pl.ds(128 * a, 128)] = band
        acc[...] += jnp.dot(lhs[...], weights[...], preferred_element_type=jnp.float32)

    scale = jnp.float32(2.0 / math.sqrt(ANGLES))
    near = lane < 64
    even = (lane & 32) == 0

    @pl.loop(0, 8)
    def _(g):
        for ty in range(2):
            for sg in range(4):
                v = [
                    acc[
                        pl.ds((ty * 4 + tx) * SLICES + sg * GROUP, GROUP),
                        pl.ds(pl.multiple_of(g * 128, 128), 128),
                    ]
                    * scale
                    for tx in range(4)
                ]
                for t in range(2):
                    p, q = v[t], v[t + 2]
                    v[t] = jnp.where(near, p, pltpu.roll(q, 64, 1))
                    v[t + 2] = jnp.where(near, pltpu.roll(p, 64, 1), q)
                for t in (0, 2):
                    p, q = v[t], v[t + 1]
                    v[t] = jnp.where(even, p, pltpu.roll(q, 32, 1))
                    v[t + 1] = jnp.where(even, pltpu.roll(p, 96, 1), q)
                for q in range(4):
                    out[TILE * ty + 4 * g + q, pl.ds(sg * GROUP, GROUP)] = v[q].astype(jnp.bfloat16)


def shards(sinogram, offsets, steps):
    rows = pl.pallas_call(
        exchange_rows,
        out_shape=jax.ShapeDtypeStruct((IMGD, GROUP, BINS // IMGD), jnp.bfloat16),
        in_specs=[VMEM],
        out_specs=VMEM,
        scratch_shapes=[
            pltpu.SemaphoreType.DMA,
            pltpu.SemaphoreType.DMA((IMGD,)),
            pltpu.SemaphoreType.DMA((IMGD,)),
        ],
        compiler_params=pltpu.CompilerParams(collective_id=0, has_side_effects=True),
        name="exchange_rows",
    )(sinogram.reshape(IMGD, GROUP, BINS // IMGD))
    packed = pl.pallas_call(
        filter_kernel,
        out_shape=jax.ShapeDtypeStruct((CHIPS, 3, GROUP, 128), jnp.bfloat16),
        in_specs=[SMEM, SMEM, VMEM],
        out_specs=VMEM,
        scratch_shapes=[
            pltpu.VMEM((64, 128, 128), jnp.bfloat16),
            pltpu.VMEM((2, 7, 128, 128), jnp.bfloat16),
            pltpu.VMEM((16, GROUP, 256), jnp.bfloat16),
            pltpu.VMEM((16, GROUP, 256), jnp.float32),
            pltpu.VMEM((36, GROUP, 128), jnp.float32),
        ],
        compiler_params=pltpu.CompilerParams(vmem_limit_bytes=LIMIT),
        name="filter_pack",
    )(offsets, steps, rows)
    windows = pl.pallas_call(
        exchange_windows,
        out_shape=jax.ShapeDtypeStruct((2, 8, IMGD, 3, GROUP, 128), jnp.bfloat16),
        in_specs=[VMEM],
        out_specs=VMEM,
        scratch_shapes=[
            pltpu.SemaphoreType.DMA,
            pltpu.SemaphoreType.DMA((CHIPS,)),
            pltpu.SemaphoreType.DMA((CHIPS,)),
            pltpu.SemaphoreType.DMA,
            pltpu.SemaphoreType.DMA,
        ],
        compiler_params=pltpu.CompilerParams(collective_id=1, has_side_effects=True, vmem_limit_bytes=LIMIT),
        name="exchange_windows",
    )(packed)
    return pl.pallas_call(
        project_kernel,
        out_shape=jax.ShapeDtypeStruct((ROWS, SLICES, COLS), jnp.bfloat16),
        in_specs=[SMEM, SMEM, VMEM],
        out_specs=VMEM,
        scratch_shapes=[
            pltpu.VMEM((8 * SLICES, 256), jnp.bfloat16),
            pltpu.VMEM((256, TILE * TILE), jnp.bfloat16),
            pltpu.VMEM((8 * SLICES, TILE * TILE), jnp.float32),
        ],
        compiler_params=pltpu.CompilerParams(vmem_limit_bytes=LIMIT),
        name="project",
    )(offsets, steps, windows.reshape(ANGLES, 4, 3, GROUP, 128))


def solution(mesh):
    return jax.shard_map(
        shards,
        mesh=mesh,
        in_specs=(P("ang", None, "img"), P(), P()),
        out_specs=P("ang", None, "img"),
        check_vma=False,
    )
```

time: 881 us -> 59.1 us (0.07)
  local copies, waits for them, and re-layouts: 390 us -> 2.31 us
  other arithmetic: 182 us -> 0 us
  matrix products: 120 us -> 0 us
  waiting for transfers between devices: 117 us -> 0 us
  Pallas kernels: 0 us -> 56.6 us
  loops' own time: 42.2 us -> 0 us
  between operations: 13.5 us -> 0.03 us
  blocking collectives: 10.1 us -> 0 us
    gather x768 -> x0, local copies, waits for them, and re-layouts: 307 us -> none
    sub x64 -> x0, other arithmetic: 121 us -> none  [the longest x32 60.5 us: one_angle(): low_bin = (position // 16 - band_start[:, None])[:, None, :]]
    dot_general x33 -> x0, matrix products: 120 us -> none  [the longest x1 76.2 us: shards(): jnp.dot(whole_bins.reshape(-1, BINS).astype(jnp.float32), ramp_rows, prec...]
    all_gather x2 -> x0, waiting for transfers between devices: 117 us -> none  [the longest x1 93.4 us: shards(): lax.all_gather(filtered, 'ang', axis=0, tiled=True)]
    min x32 -> x0, other arithmetic: 57.9 us -> none  [one_angle(): band_start = jnp.minimum(corner // 16, BINS - BAND)]
    pallas_call x0 -> x4, Pallas kernels: none -> 56.6 us  [the longest x1 22.5 us: shards(): pl.pallas_call(exchange_windows, out_shape=jax.ShapeDtypeStruct((2, 8, IM...]
    another operation x33 -> x0, loops' own time: 42.2 us -> none  [the longest x1 38.2 us: one_block(): lax.scan(one_angle, start_sum, (filtered, geo_offsets, geo_steps))[0]]
    squeeze x32 -> x0, local copies, waits for them, and re-layouts: 34.6 us -> none  [one_block(): lax.scan(one_angle, start_sum, (filtered, geo_offsets, geo_steps))[0]]
  transfers between devices with their start and end apart: 2 -> 0, of which waited for: 2 -> 0; matrix products, arithmetic and copies ran while one was open for 0% -> 0% of each run, Pallas kernels for 0% -> 0%
where the time goes in v1:
time: 59.1 us; the launch traced here: 58.9 us
  Pallas kernels  56.6 us (96%)
  local copies, waits for them, and re-layouts  2.31 us (4%)
    pallas_call x1, Pallas kernels, shards(): pl.pallas_call(exchange_windows, out_shape=jax.ShapeDtypeStruct((2, 8, IM...  22.5 us
    pallas_call x1, Pallas kernels, shards(): pl.pallas_call(project_kernel, out_shape=jax.ShapeDtypeStruct((ROWS, SLIC...  14.1 us
    pallas_call x1, Pallas kernels, shards(): pl.pallas_call(exchange_rows, out_shape=jax.ShapeDtypeStruct((IMGD, GROUP...  11.7 us
    pallas_call x1, Pallas kernels, shards(): pl.pallas_call(filter_kernel, out_shape=jax.ShapeDtypeStruct((CHIPS, 3, G...  8.26 us
    unnamed x5, local copies, waits for them, and re-layouts  2.31 us

profile of v1, /device:TPU:1, one launch (start us, length us, event | category | flops | bytes accessed | tf_op | source)
XLA Modules:
  0.0 58.9 jit_solution(1897716866625672180)
XLA Ops:
  0.0 0.8 %copy.5.steps = s32[32,2]{1,0:T(8,128)S(1)} copy(s32[32,2]{0,1:T(2,128)} %param.5) | data formatting | bytes 512 | tf_op args[2]
  0.8 11.7 %exchange_rows.1.recv = bf16[8,16,512]{2,1,0:T(8,128)(2,1)} custom-call(bf16[8,16,512]{2,1,0:T(8,128)(2,1)} %bitcast.3), custom_call_target="tpu_custom_call" | custom-call | tf_op jit(solution)/shard_map/exchange_rows/pallas_call | solution.py:261
  12.5 0.0 copy-start
  12.5 0.9 %copy-done = bf16[8,16,512]{2,1,0:T(8,128)(2,1)S(1)} copy-done((bf16[8,16,512]{2,1,0:T(8,128)(2,1)S(1)}, bf16[8,16,512]{2,1,0:T(8,128)(2,1)}, u32[]{:S(2)}) %copy-start) | copy-done | bytes 131096
  13.4 0.0 copy-start.1
  13.4 0.7 %copy-done.1 = s32[32]{0:T(128)S(1)} copy-done((s32[32]{0:T(128)S(1)}, s32[32]{0:T(128)}, u32[]{:S(2)}) %copy-start.1) | copy-done | bytes 152
  14.0 8.3 %filter_pack.1.packed = bf16[64,3,16,128]{3,2,1,0:T(8,128)(2,1)S(1)} custom-call(s32[32]{0:T(128)S(1)} %copy-done.1, s32[32,2]{1,0:T(8,128)S(1)} %copy.5.steps, bf16[8,16,512]{2,1,0:T(8,128)(2,1)S(1)} %copy-done), custom_call_target="tpu_custom_call" | custom-call | tf_op jit(solution)/shard_map/filter_pack/pallas_call | solution.py:274
  22.3 22.5 %exchange_windows.1 = bf16[2,8,8,3,16,128]{5,4,3,2,1,0:T(8,128)(2,1)S(1)} custom-call(bf16[64,3,16,128]{3,2,1,0:T(8,128)(2,1)S(1)} %filter_pack.1.packed), custom_call_target="tpu_custom_call" | custom-call | tf_op jit(solution)/shard_map/exchange_windows/pallas_call | solution.py:289
  44.8 14.1 %project.1 = bf16[64,64,128]{2,1,0:T(8,128)(2,1)} custom-call(s32[32]{0:T(128)S(1)} %copy-done.1, s32[32,2]{1,0:T(8,128)S(1)} %copy.5.steps, bf16[32,4,3,16,128]{4,3,2,1,0:T(8,128)(2,1)S(1)} %bitcast.2), custom_call_target="tpu_custom_call" | custom-call | tf_op jit(solution)/shard_map/project/pallas_call | solution.py:304
Async XLA Ops:
  12.5 0.9 %copy-start = (bf16[8,16,512]{2,1,0:T(8,128)(2,1)S(1)}, bf16[8,16,512]{2,1,0:T(8,128)(2,1)}, u32[]{:S(2)}) copy-start(bf16[8,16,512]{2,1,0:T(8,128)(2,1)} %exchange_rows.1.recv) | copy-start | bytes 393220
  13.4 0.7 %copy-start.1 = (s32[32]{0:T(128)S(1)}, s32[32]{0:T(128)}, u32[]{:S(2)}) copy-start(s32[32]{0:T(128)} %offsets.3) | copy-start | bytes 388

commit v2 on v0

v2 whole, which is shorter than its diff:
```python
import math

import jax
import jax.numpy as jnp
from jax import lax
from jax.experimental import pallas as pl
from jax.experimental.pallas import tpu as pltpu
from jax.sharding import PartitionSpec as P

BINS = 4096
IMG = 1024
ANGLES = 32
SLICES = 64
ANG = 16
IMGD = 8
CHIPS = 64
ROWS = IMG // ANG
COLS = IMG // IMGD
TILE = 32
TILES = 8
GROUP = 16
PACK = 4
MESH = pl.DeviceIdType.MESH
LIMIT = 48 * 1024 * 1024


def ramp_tiles(ramp_hi, ramp_fine):
    gap = lax.broadcasted_iota(jnp.int32, (128, 128), 1) - lax.broadcasted_iota(jnp.int32, (128, 128), 0)
    scale = jnp.where((gap & 1) != 0, jnp.float32(-1.0 / math.pi**2), jnp.float32(0.0))
    gap_f = gap.astype(jnp.float32)

    def value(e):
        t = gap_f + jnp.asarray(128 * e).astype(jnp.float32)
        t = jnp.where(t == 0.0, jnp.float32(1.0), t)
        return scale / (t * t)

    @pl.loop(0, 64)
    def _(e):
        ramp_hi[e] = value(e - 32).astype(jnp.bfloat16)

    for e in range(-3, 4):
        v = value(e)
        if e == 0:
            v = jnp.where(gap == 0, jnp.float32(0.25), v)
        hi = v.astype(jnp.bfloat16)
        rest = v - hi.astype(jnp.float32)
        mid = rest.astype(jnp.bfloat16)
        low = (rest - mid.astype(jnp.float32)).astype(jnp.bfloat16)
        ramp_hi[e + 32] = hi
        ramp_fine[0, e + 3] = mid
        ramp_fine[1, e + 3] = low


def toeplitz(tiles, at):
    top = jnp.concatenate([tiles[at], tiles[at + 1]], axis=1)
    low = jnp.concatenate([tiles[at - 1], tiles[at]], axis=1)
    return jnp.concatenate([top, low], axis=0)


def filter_rows(rows, acc, filt, ramp_hi, ramp_fine):
    for d in sorted(range(-15, 16), key=abs):
        count = 16 - abs(d)
        first = max(0, -d)
        lhs = jnp.concatenate(
            [rows[b // 2, :, pl.ds(256 * (b % 2), 256)] for b in range(first, first + count)], axis=0
        )
        total = jnp.dot(lhs, toeplitz(ramp_hi, 2 * d + 32), preferred_element_type=jnp.float32)
        if abs(d) <= 1:
            for term in range(2):
                total += jnp.dot(
                    lhs, toeplitz(ramp_fine.at[term], 2 * d + 3), preferred_element_type=jnp.float32
                )
        total = total.reshape(count, GROUP, 256)
        if d == 0:
            acc[...] = total
        else:
            acc[pl.ds(max(0, d), count)] += total
    for b in range(16):
        for h in range(2):
            filt[2 * b + h] = acc[b, :, pl.ds(128 * h, 128)].astype(jnp.bfloat16)
    filt[pl.ds(32, 4)] = jnp.zeros((4, GROUP, 128), jnp.bfloat16)


def angle_data(offsets, steps, a):
    u = steps[0, a]
    v = steps[1, a]
    return offsets[a], u, v, jnp.minimum(u, 0) + jnp.minimum(v, 0)


def window_start(offset, u, v, low, chip_row, img):
    return (offset + u * (COLS * img) + v * (2 * ROWS * chip_row) + low * 127) >> 4


def place_lhs(part, lhs, offsets, steps, angle_of):
    i = lax.axis_index("ang")
    j = lax.axis_index("img")
    lane = lax.broadcasted_iota(jnp.int32, (1, 128), 1)

    @pl.loop(0, 4)
    def _(q):
        for a in range(2):
            offset, u, v, low = angle_data(offsets, steps, angle_of(q, a))
            ws = window_start(offset, u, v, low, i // 2, j)
            for tile in range(TILES):
                ty, tx = tile // 4, tile % 4
                corner = offset + u * (COLS * j + TILE * tx) + v * (ROWS * i + TILE * ty) + low * (TILE - 1)
                begin = (corner >> 4) - ws
                block = begin >> 7
                shift = begin & 127
                back = (128 - shift) & 127
                after = jnp.minimum(block + 1, 2)
                left = part[q, pl.ds(4 * a, 4), block].reshape(SLICES, 128)
                right = part[q, pl.ds(4 * a, 4), after].reshape(SLICES, 128)
                left = pltpu.roll(left, back, 1)
                right = pltpu.roll(right, back, 1)
                band = jnp.where(lane < 128 - shift, left, right)
                lhs[q, pl.ds(tile * SLICES, SLICES), pl.ds(128 * a, 128)] = band


def store_picture(acc, out):
    lane = lax.broadcasted_iota(jnp.int32, (1, 128), 1)
    scale = jnp.float32(2.0 / math.sqrt(ANGLES))
    near = lane < 64
    even = (lane & 32) == 0

    @pl.loop(0, 8)
    def _(g):
        at = pl.ds(pl.multiple_of(g * 128, 128), 128)
        for ty in range(2):
            v = [
                (acc[pl.ds((ty * 4 + tx) * SLICES, SLICES), at] * scale).astype(jnp.bfloat16) for tx in range(4)
            ]
            for t in range(2):
                p, q = v[t], v[t + 2]
                v[t] = jnp.where(near, p, pltpu.roll(q, 64, 1))
                v[t + 2] = jnp.where(near, pltpu.roll(p, 64, 1), q)
            for t in (0, 2):
                p, q = v[t], v[t + 1]
                v[t] = jnp.where(even, p, pltpu.roll(q, 32, 1))
                v[t + 1] = jnp.where(even, pltpu.roll(p, 96, 1), q)
            for q in range(4):
                out[TILE * ty + 4 * g + q] = v[q]


def whole_kernel(
    offsets,
    steps,
    sino,
    out,
    rows,
    packed,
    own_a,
    own_b,
    sib_a,
    sib_b,
    ramp_hi,
    ramp_fine,
    filt_acc,
    filt,
    weights,
    lhs,
    acc,
    local_sem,
    row_send,
    row_recv,
    win_send,
    win_recv,
    sib_send,
    sib_recv,
):
    i = lax.axis_index("ang")
    j = lax.axis_index("img")
    core = lax.rem(i, 2)
    row = i // 2

    def partner(k):
        return lax.rem(row + k // IMGD, IMGD), lax.rem(j + lax.rem(k, IMGD), IMGD)

    barrier = pltpu.get_barrier_semaphore()
    own_rows = pltpu.make_async_copy(sino.at[j], rows.at[j], local_sem)
    own_rows.start()

    @pl.loop(1, CHIPS)
    def _(k):
        r, c = partner(k)
        pl.semaphore_signal(barrier, inc=1, device_id=(2 * r + core, c), device_id_type=MESH)

    sibling = (i + 1 - 2 * core, j)
    pl.semaphore_signal(barrier, inc=1, device_id=sibling, device_id_type=MESH)

    ramp_tiles(ramp_hi, ramp_fine)
    pl.semaphore_wait(barrier, CHIPS)

    def row_copy(k):
        to = lax.rem(j + k, IMGD)
        return pltpu.make_async_remote_copy(
            src_ref=sino.at[to],
            dst_ref=rows.at[j],
            send_sem=row_send.at[k],
            recv_sem=row_recv.at[k],
            device_id=(i, to),
            device_id_type=MESH,
        )

    row_copies = [row_copy(k) for k in range(1, IMGD)]
    for c in row_copies:
        c.start()

    def source_angle(q, a, stage):
        back, whose = stage // 2, stage % 2
        chip = lax.rem(row - (q + 4 * back) + IMGD, IMGD)
        side = core if whose == 0 else 1 - core
        return 4 * chip + 2 * side + a

    pixel = lax.broadcasted_iota(jnp.int32, (1, TILE * TILE), 1)
    px = (pixel & (TILE - 1)).astype(jnp.float32) * 0.0625
    py = (pixel >> 5).astype(jnp.float32) * 0.0625
    slot = lax.broadcasted_iota(jnp.int32, (128, TILE * TILE), 0).astype(jnp.float32)
    for stage in range(4):

        @pl.loop(0, 4)
        def _(q):
            for a in range(2):
                offset, u, v, low = angle_data(offsets, steps, source_angle(q, a, stage))
                first = ((offset + low * (TILE - 1)) & 15) - low * (TILE - 1)
                where = (
                    first.astype(jnp.float32) * 0.0625 + u.astype(jnp.float32) * px + v.astype(jnp.float32) * py
                )
                weights[stage, q, pl.ds(128 * a, 128)] = jnp.maximum(1.0 - jnp.abs(slot - where), 0.0).astype(
                    jnp.bfloat16
                )

    own_rows.wait()
    for c in row_copies:
        c.wait()
    filter_rows(rows, filt_acc, filt, ramp_hi, ramp_fine)

    offset, u, v, low = angle_data(offsets, steps, 2 * i + j // 4)
    lane = lax.broadcasted_iota(jnp.int32, (1, 128), 1)

    def pack(k):
        r, c = partner(k)
        ws = window_start(offset, u, v, low, r, c)
        shift = ws & 127
        back = (128 - shift) & 127
        blocks = filt[pl.ds(ws >> 7, 4)]
        rolled = [pltpu.roll(blocks[n], back, 1) for n in range(4)]
        return [jnp.where(lane < 128 - shift, rolled[n], rolled[n + 1]) for n in range(3)]

    def window_copy(k, own, back):
        r, c = partner(k)
        return pltpu.make_async_remote_copy(
            src_ref=packed.at[k],
            dst_ref=own.at[k // IMGD - 4 * back, j],
            send_sem=win_send.at[k],
            recv_sem=win_recv.at[k],
            device_id=(2 * r + core, c),
            device_id_type=MESH,
        )

    def send(ks, own, back):
        for k in ks:
            for n, block in enumerate(pack(k)):
                packed[k, n] = block
        for k in ks:
            window_copy(k, own, back).start()

    for n, block in enumerate(pack(0)):
        own_a[0, j, n] = block
    send([1, 2, 3], own_a, 0)

    @pl.loop(1, 32 // PACK)
    def _(t):
        send([PACK * t + n for n in range(PACK)], own_a, 0)

    @pl.loop(32 // PACK, 64 // PACK)
    def _(t):
        send([PACK * t + n for n in range(PACK)], own_b, 1)

    def share_copy(own, sib, back):
        return pltpu.make_async_remote_copy(
            src_ref=own,
            dst_ref=sib,
            send_sem=sib_send.at[back],
            recv_sem=sib_recv.at[back],
            device_id=sibling,
            device_id_type=MESH,
        )

    def project(stage, part):
        place_lhs(part, lhs, offsets, steps, lambda q, a: source_angle(q, a, stage))
        left = jnp.concatenate([lhs[q] for q in range(4)], axis=1)
        right = weights[stage].reshape(4 * 256, TILE * TILE)
        total = jnp.dot(left, right, preferred_element_type=jnp.float32)
        if stage == 0:
            acc[...] = total
        else:
            acc[...] += total

    @pl.loop(1, 32)
    def _(k):
        window_copy(k, own_a, 0).wait_recv()

    share_a = share_copy(own_a, sib_a, 0)
    share_a.start()
    project(0, own_a)

    @pl.loop(32, 64)
    def _(k):
        window_copy(k, own_b, 1).wait_recv()

    share_b = share_copy(own_b, sib_b, 1)
    share_b.start()
    share_a.wait_recv()
    project(1, sib_a)
    project(2, own_b)
    share_b.wait_recv()
    project(3, sib_b)
    store_picture(acc, out)
    share_a.wait_send()
    share_b.wait_send()

    @pl.loop(1, 32)
    def _(k):
        window_copy(k, own_a, 0).wait_send()

    @pl.loop(32, 64)
    def _(k):
        window_copy(k, own_b, 1).wait_send()


def shards(sinogram, offsets, steps):
    vmem = pl.BlockSpec(memory_space=pltpu.VMEM)
    smem = pl.BlockSpec(memory_space=pltpu.SMEM)
    window = (3, GROUP, 128)
    return pl.pallas_call(
        whole_kernel,
        out_shape=jax.ShapeDtypeStruct((ROWS, SLICES, COLS), jnp.bfloat16),
        in_specs=[smem, smem, vmem],
        out_specs=vmem,
        scratch_shapes=[
            pltpu.VMEM((IMGD, GROUP, BINS // IMGD), jnp.bfloat16),
            pltpu.VMEM((CHIPS, *window), jnp.bfloat16),
            pltpu.VMEM((4, IMGD, *window), jnp.bfloat16),
            pltpu.VMEM((4, IMGD, *window), jnp.bfloat16),
            pltpu.VMEM((4, IMGD, *window), jnp.bfloat16),
            pltpu.VMEM((4, IMGD, *window), jnp.bfloat16),
            pltpu.VMEM((64, 128, 128), jnp.bfloat16),
            pltpu.VMEM((2, 7, 128, 128), jnp.bfloat16),
            pltpu.VMEM((16, GROUP, 256), jnp.float32),
            pltpu.VMEM((36, GROUP, 128), jnp.bfloat16),
            pltpu.VMEM((4, 4, 256, TILE * TILE), jnp.bfloat16),
            pltpu.VMEM((4, TILES * SLICES, 256), jnp.bfloat16),
            pltpu.VMEM((TILES * SLICES, TILE * TILE), jnp.float32),
            pltpu.SemaphoreType.DMA,
            pltpu.SemaphoreType.DMA((IMGD,)),
            pltpu.SemaphoreType.DMA((IMGD,)),
            pltpu.SemaphoreType.DMA((CHIPS,)),
            pltpu.SemaphoreType.DMA((CHIPS,)),
            pltpu.SemaphoreType.DMA((2,)),
            pltpu.SemaphoreType.DMA((2,)),
        ],
        compiler_params=pltpu.CompilerParams(collective_id=0, has_side_effects=True, vmem_limit_bytes=LIMIT),
        name="back_projection",
    )(offsets, steps.T, sinogram.reshape(IMGD, GROUP, BINS // IMGD))


def solution(mesh):
    return jax.shard_map(
        shards,
        mesh=mesh,
        in_specs=(P("ang", None, "img"), P(), P()),
        out_specs=P("ang", None, "img"),
        check_vma=False,
    )
```

time: 881 us -> 45.1 us (0.05)
  the two profiles are of different devices: /device:TPU:1 before, /device:TPU:0 now
where the time goes in v2:
time: 45.1 us; the launch traced here: 45 us
  Pallas kernels  42.4 us (94%)
  local copies, waits for them, and re-layouts  2.56 us (6%)
    pallas_call x1, Pallas kernels, shards(): pl.pallas_call(whole_kernel, out_shape=jax.ShapeDtypeStruct((ROWS, SLICES...  42.4 us
    unnamed x7, local copies, waits for them, and re-layouts  2.56 us

profile of v2, /device:TPU:0, one launch (start us, length us, event | category | flops | bytes accessed | tf_op | source)
XLA Modules:
  0.0 45.0 jit_solution(5164496044383250757)
XLA Ops:
  0.0 0.0 copy-start.1
  0.0 0.0 copy-start.2
  0.0 0.7 %copy-done.1 = s32[32,2]{0,1:T(2,128)S(1)} copy-done((s32[32,2]{0,1:T(2,128)S(1)}, s32[32,2]{0,1:T(2,128)}, u32[]{:S(2)}) %copy-start.1) | copy-done | bytes 280
  0.7 0.0 copy-done.2
  0.7 0.0 copy-start
  0.7 0.9 %copy-done = bf16[2,64,512]{2,1,0:T(8,128)(2,1)S(1)} copy-done((bf16[2,64,512]{2,1,0:T(8,128)(2,1)S(1)}, bf16[2,64,512]{2,1,0:T(8,128)(2,1)}, u32[]{:S(2)}) %copy-start) | copy-done | bytes 131096
  1.6 42.4 %back_projection.1 = bf16[64,64,128]{2,1,0:T(8,128)(2,1)S(1)} custom-call(s32[32]{0:T(128)S(1)} %copy-done.2, s32[2,32]{1,0:T(2,128)S(1)} %bitcast.3, bf16[8,16,512]{2,1,0:T(8,128)(2,1)S(1)} %bitcast.2), custom_call_target="tpu_custom_call" | custom-call | tf_op jit(solution)/shard_map/back_projection/pallas_call | solution.py:336
  44.0 1.0 %copy.5 = bf16[64,64,128]{2,1,0:T(8,128)(2,1)} copy(bf16[64,64,128]{2,1,0:T(8,128)(2,1)S(1)} %back_projection.1) | data formatting | bytes 2097152
Async XLA Ops:
  0.0 0.7 %copy-start.1 = (s32[32,2]{0,1:T(2,128)S(1)}, s32[32,2]{0,1:T(2,128)}, u32[]{:S(2)}) copy-start(s32[32,2]{0,1:T(2,128)} %param.5) | copy-start | bytes 772
  0.0 0.7 %copy-start.2 = (s32[32]{0:T(128)S(1)}, s32[32]{0:T(128)}, u32[]{:S(2)}) copy-start(s32[32]{0:T(128)} %offsets.1) | copy-start | bytes 388
  0.7 0.9 %copy-start = (bf16[2,64,512]{2,1,0:T(8,128)(2,1)S(1)}, bf16[2,64,512]{2,1,0:T(8,128)(2,1)}, u32[]{:S(2)}) copy-start(bf16[2,64,512]{2,1,0:T(8,128)(2,1)} %param.3) | copy-start | bytes 393220

commit v3 on v2

v3 whole, which is shorter than its diff:
```python
import math

import jax
import jax.numpy as jnp
from jax import lax
from jax.experimental import pallas as pl
from jax.experimental.pallas import tpu as pltpu
from jax.sharding import PartitionSpec as P

BINS = 4096
IMG = 1024
ANGLES = 32
SLICES = 64
ANG = 16
IMGD = 8
ROWS = IMG // ANG
COLS = IMG // IMGD
TILE = 32
TILES = 8
GROUP = 16
MESH = pl.DeviceIdType.MESH
LIMIT = 48 * 1024 * 1024


def ramp_tiles(ramp_hi, ramp_fine):
    gap = lax.broadcasted_iota(jnp.int32, (128, 128), 1) - lax.broadcasted_iota(jnp.int32, (128, 128), 0)
    scale = jnp.where((gap & 1) != 0, jnp.float32(-1.0 / math.pi**2), jnp.float32(0.0))
    gap_f = gap.astype(jnp.float32)

    def value(e):
        t = gap_f + jnp.asarray(128 * e).astype(jnp.float32)
        t = jnp.where(t == 0.0, jnp.float32(1.0), t)
        return scale / (t * t)

    @pl.loop(0, 64)
    def _(e):
        ramp_hi[e] = value(e - 32).astype(jnp.bfloat16)

    for e in range(-3, 4):
        v = value(e)
        if e == 0:
            v = jnp.where(gap == 0, jnp.float32(0.25), v)
        hi = v.astype(jnp.bfloat16)
        rest = v - hi.astype(jnp.float32)
        mid = rest.astype(jnp.bfloat16)
        low = (rest - mid.astype(jnp.float32)).astype(jnp.bfloat16)
        ramp_hi[e + 32] = hi
        ramp_fine[0, e + 3] = mid
        ramp_fine[1, e + 3] = low


def toeplitz(tiles, at):
    top = jnp.concatenate([tiles[at], tiles[at + 1]], axis=1)
    low = jnp.concatenate([tiles[at - 1], tiles[at]], axis=1)
    return jnp.concatenate([top, low], axis=0)


def filter_rows(rows, acc, filt, ramp_hi, ramp_fine):
    for d in sorted(range(-15, 16), key=abs):
        count = 16 - abs(d)
        first = max(0, -d)
        lhs = jnp.concatenate(
            [rows[b // 2, :, pl.ds(256 * (b % 2), 256)] for b in range(first, first + count)], axis=0
        )
        total = jnp.dot(lhs, toeplitz(ramp_hi, 2 * d + 32), preferred_element_type=jnp.float32)
        if abs(d) <= 1:
            for term in range(2):
                total += jnp.dot(
                    lhs, toeplitz(ramp_fine.at[term], 2 * d + 3), preferred_element_type=jnp.float32
                )
        total = total.reshape(count, GROUP, 256)
        if d == 0:
            acc[...] = total
        else:
            acc[pl.ds(max(0, d), count)] += total
    for b in range(16):
        for h in range(2):
            filt[2 * b + h] = acc[b, :, pl.ds(128 * h, 128)].astype(jnp.bfloat16)
    filt[pl.ds(32, 4)] = jnp.zeros((4, GROUP, 128), jnp.bfloat16)


def angle_data(offsets, steps, a):
    u = steps[0, a]
    v = steps[1, a]
    return offsets[a], u, v, jnp.minimum(u, 0) + jnp.minimum(v, 0)


def window_start(offset, u, v, low, chip_row, img):
    return (offset + u * (COLS * img) + v * (2 * ROWS * chip_row) + low * 127) >> 4


def place_lhs(part, lhs, offsets, steps, angle_of):
    i = lax.axis_index("ang")
    j = lax.axis_index("img")
    lane = lax.broadcasted_iota(jnp.int32, (1, 128), 1)
    for q in range(2):
        for a in range(2):
            offset, u, v, low = angle_data(offsets, steps, angle_of(q, a))
            ws = window_start(offset, u, v, low, i >> 1, j)
            base = offset + u * (COLS * j) + v * (ROWS * i) + low * (TILE - 1)
            for tile in range(TILES):
                ty, tx = tile // 4, tile % 4
                begin = ((base + u * (TILE * tx) + v * (TILE * ty)) >> 4) - ws
                block = begin >> 7
                shift = begin & 127
                back = (128 - shift) & 127
                after = jnp.minimum(block + 1, 2)
                left = part[q, pl.ds(4 * a, 4), block].reshape(SLICES, 128)
                right = part[q, pl.ds(4 * a, 4), after].reshape(SLICES, 128)
                left = pltpu.roll(left, back, 1)
                right = pltpu.roll(right, back, 1)
                band = jnp.where(lane < 128 - shift, left, right)
                lhs[pl.ds(tile * SLICES, SLICES), pl.ds(256 * q + 128 * a, 128)] = band


def store_picture(acc, out):
    lane = lax.broadcasted_iota(jnp.int32, (1, 128), 1)
    scale = jnp.float32(2.0 / math.sqrt(ANGLES))
    near = lane < 64
    even = (lane & 32) == 0

    @pl.loop(0, 8)
    def _(g):
        at = pl.ds(pl.multiple_of(g * 128, 128), 128)
        for ty in range(2):
            v = [
                (acc[pl.ds((ty * 4 + tx) * SLICES, SLICES), at] * scale).astype(jnp.bfloat16) for tx in range(4)
            ]
            for t in range(2):
                p, q = v[t], v[t + 2]
                v[t] = jnp.where(near, p, pltpu.roll(q, 64, 1))
                v[t + 2] = jnp.where(near, pltpu.roll(p, 64, 1), q)
            for t in (0, 2):
                p, q = v[t], v[t + 1]
                v[t] = jnp.where(even, p, pltpu.roll(q, 32, 1))
                v[t + 1] = jnp.where(even, pltpu.roll(p, 96, 1), q)
            for q in range(4):
                out[TILE * ty + 4 * g + q] = v[q]


def whole_kernel(
    offsets_in,
    steps_in,
    sino,
    out,
    offsets,
    steps,
    rows,
    packed,
    own_0,
    own_1,
    own_2,
    own_3,
    sib_0,
    sib_1,
    sib_2,
    sib_3,
    ramp_hi,
    ramp_fine,
    filt_acc,
    filt,
    weights,
    lhs_0,
    lhs_1,
    acc,
    local_sem,
    row_send,
    row_recv,
    win_send,
    win_recv,
    sib_send,
    sib_recv,
):
    i = lax.axis_index("ang")
    j = lax.axis_index("img")
    core = i & 1
    row = i >> 1
    sibling = (i + 1 - 2 * core, j)
    own = (own_0, own_1, own_2, own_3)
    sib = (sib_0, sib_1, sib_2, sib_3)

    barrier = pltpu.get_barrier_semaphore()
    for k in range(1, IMGD):
        pl.semaphore_signal(barrier, inc=1, device_id=(i, (j + k) & 7), device_id_type=MESH)
    for k in range(1, IMGD):
        pl.semaphore_signal(barrier, inc=1, device_id=((i + 2 * k) & 15, j), device_id_type=MESH)
    pl.semaphore_signal(barrier, inc=1, device_id=sibling, device_id_type=MESH)
    local = [
        pltpu.make_async_copy(offsets_in, offsets, local_sem.at[0]),
        pltpu.make_async_copy(steps_in, steps, local_sem.at[1]),
        pltpu.make_async_copy(sino.at[j], rows.at[j], local_sem.at[2]),
    ]
    for c in local:
        c.start()
    pl.semaphore_wait(barrier, 15)

    def row_copy(k):
        to = (j + k) & 7
        return pltpu.make_async_remote_copy(
            src_ref=sino.at[to],
            dst_ref=rows.at[j],
            send_sem=row_send.at[k],
            recv_sem=row_recv.at[k],
            device_id=(i, to),
            device_id_type=MESH,
        )

    row_copies = [row_copy(k) for k in range(1, IMGD)]
    for c in row_copies:
        c.start()
    for c in local:
        c.wait()
    ramp_tiles(ramp_hi, ramp_fine)

    def source_angle(stage, q, a):
        chip = (row - (2 * (stage >> 1) + q)) & 7
        side = core ^ (stage & 1)
        return 4 * chip + 2 * side + a

    pixel = lax.broadcasted_iota(jnp.int32, (1, TILE * TILE), 1)
    px = (pixel & (TILE - 1)).astype(jnp.float32) * 0.0625
    py = (pixel >> 5).astype(jnp.float32) * 0.0625
    slot = lax.broadcasted_iota(jnp.int32, (128, TILE * TILE), 0).astype(jnp.float32)

    @pl.loop(0, 8)
    def _(stage):
        for q in range(2):
            for a in range(2):
                offset, u, v, low = angle_data(offsets, steps, source_angle(stage, q, a))
                first = ((offset + low * (TILE - 1)) & 15) - low * (TILE - 1)
                where = (
                    first.astype(jnp.float32) * 0.0625 + u.astype(jnp.float32) * px + v.astype(jnp.float32) * py
                )
                weights[stage, pl.ds(256 * q + 128 * a, 128)] = jnp.maximum(
                    1.0 - jnp.abs(slot - where), 0.0
                ).astype(jnp.bfloat16)

    for c in row_copies:
        c.wait_recv()
    filter_rows(rows, filt_acc, filt, ramp_hi, ramp_fine)

    offset, u, v, low = angle_data(offsets, steps, 2 * i + (j >> 2))
    lane = lax.broadcasted_iota(jnp.int32, (1, 128), 1)

    def pack(r, c):
        ws = window_start(offset, u, v, low, r, c)
        shift = ws & 127
        back = (128 - shift) & 127
        blocks = filt[pl.ds(ws >> 7, 4)]
        rolled = [pltpu.roll(blocks[n], back, 1) for n in range(4)]
        return [jnp.where(lane < 128 - shift, rolled[n], rolled[n + 1]) for n in range(3)]

    def window_copy(group, k, part, q):
        r = (row + group) & 7
        c = (j + k) & 7
        return pltpu.make_async_remote_copy(
            src_ref=packed.at[group, k],
            dst_ref=part.at[q, j],
            send_sem=win_send.at[group],
            recv_sem=win_recv.at[group],
            device_id=(2 * r + core, c),
            device_id_type=MESH,
        )

    def group_copy(group, part, q, count):
        return pltpu.make_async_remote_copy(
            src_ref=packed.at[group, pl.ds(IMGD - count, count)],
            dst_ref=part.at[q, pl.ds(0, count)],
            send_sem=win_send.at[group],
            recv_sem=win_recv.at[group],
            device_id=sibling,
            device_id_type=MESH,
        )

    for n, block in enumerate(pack(row, j)):
        own_0[0, j, n] = block
    for group in range(8):
        r = (row + group) & 7
        ks = range(1 if group == 0 else 0, IMGD)
        for half in (ks[: len(ks) // 2], ks[len(ks) // 2 :]):
            for k in half:
                for n, block in enumerate(pack(r, (j + k) & 7)):
                    packed[group, k, n] = block
            for k in half:
                window_copy(group, k, own[group // 2], group % 2).start()

    def group_waits(p):
        return [group_copy(2 * p + q, own[p], q, 7 if 2 * p + q == 0 else 8) for q in range(2)]

    def share_copy(p):
        return pltpu.make_async_remote_copy(
            src_ref=own[p],
            dst_ref=sib[p],
            send_sem=sib_send.at[p],
            recv_sem=sib_recv.at[p],
            device_id=sibling,
            device_id_type=MESH,
        )

    def arrive(p):
        for c in group_waits(p):
            c.wait_recv()
        share_copy(p).start()

    def prepare(stage, n):
        p = stage // 2
        place_lhs(
            (own if stage % 2 == 0 else sib)[p],
            (lhs_0, lhs_1)[n % 2],
            offsets,
            steps,
            lambda q, a: source_angle(stage, q, a),
        )

    order = (0, 2, 1, 4, 3, 6, 5, 7)
    arrive(0)
    prepare(0, 0)
    for n, stage in enumerate(order):
        if n + 1 < 8:
            after = order[n + 1]
            if after in (2, 4, 6):
                arrive(after // 2)
            if after % 2 == 1:
                share_copy(after // 2).wait_recv()
            prepare(after, n + 1)
        total = jnp.dot((lhs_0, lhs_1)[n % 2][...], weights[stage], preferred_element_type=jnp.float32)
        if n == 0:
            acc[...] = total
        else:
            acc[...] += total
    store_picture(acc, out)
    for c in row_copies:
        c.wait_send()
    for p in range(4):
        share_copy(p).wait_send()
        for c in group_waits(p):
            c.wait_send()


def shards(sinogram, offsets, steps):
    vmem = pl.BlockSpec(memory_space=pltpu.VMEM)
    hbm = pl.BlockSpec(memory_space=pl.ANY)
    window = (3, GROUP, 128)
    return pl.pallas_call(
        whole_kernel,
        out_shape=jax.ShapeDtypeStruct((ROWS, SLICES, COLS), jnp.bfloat16),
        in_specs=[hbm, hbm, hbm],
        out_specs=vmem,
        scratch_shapes=[
            pltpu.SMEM((ANGLES,), jnp.int32),
            pltpu.SMEM((2, ANGLES), jnp.int32),
            pltpu.VMEM((IMGD, GROUP, BINS // IMGD), jnp.bfloat16),
            pltpu.VMEM((8, IMGD, *window), jnp.bfloat16),
            *([pltpu.VMEM((2, IMGD, *window), jnp.bfloat16)] * 8),
            pltpu.VMEM((64, 128, 128), jnp.bfloat16),
            pltpu.VMEM((2, 7, 128, 128), jnp.bfloat16),
            pltpu.VMEM((16, GROUP, 256), jnp.float32),
            pltpu.VMEM((36, GROUP, 128), jnp.bfloat16),
            pltpu.VMEM((8, 512, TILE * TILE), jnp.bfloat16),
            pltpu.VMEM((TILES * SLICES, 512), jnp.bfloat16),
            pltpu.VMEM((TILES * SLICES, 512), jnp.bfloat16),
            pltpu.VMEM((TILES * SLICES, TILE * TILE), jnp.float32),
            pltpu.SemaphoreType.DMA((3,)),
            pltpu.SemaphoreType.DMA((IMGD,)),
            pltpu.SemaphoreType.DMA((IMGD,)),
            pltpu.SemaphoreType.DMA((8,)),
            pltpu.SemaphoreType.DMA((8,)),
            pltpu.SemaphoreType.DMA((4,)),
            pltpu.SemaphoreType.DMA((4,)),
        ],
        compiler_params=pltpu.CompilerParams(collective_id=0, has_side_effects=True, vmem_limit_bytes=LIMIT),
        name="back_projection",
    )(offsets, steps.T, sinogram.reshape(IMGD, GROUP, BINS // IMGD))


def solution(mesh):
    return jax.shard_map(
        shards,
        mesh=mesh,
        in_specs=(P("ang", None, "img"), P(), P()),
        out_specs=P("ang", None, "img"),
        check_vma=False,
    )
```

time: 45.1 us -> 38.5 us (0.85)
  the two profiles are of different devices: /device:TPU:0 before, /device:TPU:1 now
where the time goes in v3:
time: 38.5 us; the launch traced here: 38.2 us
  Pallas kernels  35.6 us (92%)
  local copies, waits for them, and re-layouts  2.56 us (7%)
    pallas_call x1, Pallas kernels, shards(): pl.pallas_call(whole_kernel, out_shape=jax.ShapeDtypeStruct((ROWS, SLICES...  35.6 us
    unnamed x7, local copies, waits for them, and re-layouts  2.56 us

profile of v3, /device:TPU:1, one launch (start us, length us, event | category | flops | bytes accessed | tf_op | source)
XLA Modules:
  0.0 38.2 jit_solution(99460449190027782)
XLA Ops:
  0.0 0.0 copy-start.1
  0.0 0.0 copy-start.2
  0.0 0.7 %copy-done.1 = s32[32,2]{0,1:T(2,128)S(1)} copy-done((s32[32,2]{0,1:T(2,128)S(1)}, s32[32,2]{0,1:T(2,128)}, u32[]{:S(2)}) %copy-start.1) | copy-done | bytes 280
  0.7 0.0 copy-done.2
  0.7 0.0 copy-start
  0.7 0.9 %copy-done = bf16[2,64,512]{2,1,0:T(8,128)(2,1)S(1)} copy-done((bf16[2,64,512]{2,1,0:T(8,128)(2,1)S(1)}, bf16[2,64,512]{2,1,0:T(8,128)(2,1)}, u32[]{:S(2)}) %copy-start) | copy-done | bytes 131096
  1.6 35.6 %back_projection.1 = bf16[64,64,128]{2,1,0:T(8,128)(2,1)S(1)} custom-call(s32[32]{0:T(128)S(1)} %copy-done.2, s32[2,32]{1,0:T(2,128)S(1)} %bitcast.3, bf16[8,16,512]{2,1,0:T(8,128)(2,1)S(1)} %bitcast.2), custom_call_target="tpu_custom_call" | custom-call | tf_op jit(solution)/shard_map/back_projection/pallas_call | solution.py:344
  37.2 1.0 %copy.5 = bf16[64,64,128]{2,1,0:T(8,128)(2,1)} copy(bf16[64,64,128]{2,1,0:T(8,128)(2,1)S(1)} %back_projection.1) | data formatting | bytes 2097152
Async XLA Ops:
  0.0 0.7 %copy-start.1 = (s32[32,2]{0,1:T(2,128)S(1)}, s32[32,2]{0,1:T(2,128)}, u32[]{:S(2)}) copy-start(s32[32,2]{0,1:T(2,128)} %param.5) | copy-start | bytes 772
  0.0 0.7 %copy-start.2 = (s32[32]{0:T(128)S(1)}, s32[32]{0:T(128)}, u32[]{:S(2)}) copy-start(s32[32]{0:T(128)} %offsets_in.1) | copy-start | bytes 388
  0.7 0.9 %copy-start = (bf16[2,64,512]{2,1,0:T(8,128)(2,1)S(1)}, bf16[2,64,512]{2,1,0:T(8,128)(2,1)}, u32[]{:S(2)}) copy-start(bf16[2,64,512]{2,1,0:T(8,128)(2,1)} %param.3) | copy-start | bytes 393220

commit v4 on v3

--- a/solution.py
+++ b/solution.py
@@ -93,38 +93,36 @@
     i = lax.axis_index("ang")
     j = lax.axis_index("img")
     lane = lax.broadcasted_iota(jnp.int32, (1, 128), 1)
-    for q in range(2):
-        for a in range(2):
-            offset, u, v, low = angle_data(offsets, steps, angle_of(q, a))
-            ws = window_start(offset, u, v, low, i >> 1, j)
-            base = offset + u * (COLS * j) + v * (ROWS * i) + low * (TILE - 1)
-            for tile in range(TILES):
-                ty, tx = tile // 4, tile % 4
-                begin = ((base + u * (TILE * tx) + v * (TILE * ty)) >> 4) - ws
-                block = begin >> 7
-                shift = begin & 127
-                back = (128 - shift) & 127
-                after = jnp.minimum(block + 1, 2)
-                left = part[q, pl.ds(4 * a, 4), block].reshape(SLICES, 128)
-                right = part[q, pl.ds(4 * a, 4), after].reshape(SLICES, 128)
-                left = pltpu.roll(left, back, 1)
-                right = pltpu.roll(right, back, 1)
-                band = jnp.where(lane < 128 - shift, left, right)
-                lhs[pl.ds(tile * SLICES, SLICES), pl.ds(256 * q + 128 * a, 128)] = band
-
-
-def store_picture(acc, out):
+    for dx in range(4):
+        offset, u, v, low = angle_data(offsets, steps, angle_of(dx))
+        ws = window_start(offset, u, v, low, i >> 1, j)
+        base = offset + u * (COLS * j) + v * (ROWS * i) + low * (TILE - 1)
+        for tile in range(TILES):
+            ty, tx = tile // 4, tile % 4
+            begin = ((base + u * (TILE * tx) + v * (TILE * ty)) >> 4) - ws
+            block = begin >> 7
+            shift = begin & 127
+            back = (128 - shift) & 127
+            after = jnp.minimum(block + 1, 2)
+            left = part[pl.ds(4 * dx, 4), block].reshape(SLICES, 128)
+            right = part[pl.ds(4 * dx, 4), after].reshape(SLICES, 128)
+            left = pltpu.roll(left, back, 1)
+            right = pltpu.roll(right, back, 1)
+            band = jnp.where(lane < 128 - shift, left, right)
+            lhs[pl.ds(tile * SLICES, SLICES), pl.ds(128 * dx, 128)] = band
+
+
+def store_rows(values, out, first):
     lane = lax.broadcasted_iota(jnp.int32, (1, 128), 1)
     scale = jnp.float32(2.0 / math.sqrt(ANGLES))
     near = lane < 64
     even = (lane & 32) == 0
-
-    @pl.loop(0, 8)
-    def _(g):
-        at = pl.ds(pl.multiple_of(g * 128, 128), 128)
+    values = (values * scale).astype(jnp.bfloat16)
+    for g in range(values.shape[1] // 128):
         for ty in range(2):
             v = [
-                (acc[pl.ds((ty * 4 + tx) * SLICES, SLICES), at] * scale).astype(jnp.bfloat16) for tx in range(4)
+                values[(ty * 4 + tx) * SLICES : (ty * 4 + tx + 1) * SLICES, g * 128 : g * 128 + 128]
+                for tx in range(4)
             ]
             for t in range(2):
                 p, q = v[t], v[t + 2]
@@ -135,7 +133,7 @@
                 v[t] = jnp.where(even, p, pltpu.roll(q, 32, 1))
                 v[t + 1] = jnp.where(even, pltpu.roll(p, 96, 1), q)
             for q in range(4):
-                out[TILE * ty + 4 * g + q] = v[q]
+                out[TILE * ty + first + 4 * g + q] = v[q]
 
 
 def whole_kernel(
@@ -175,6 +173,7 @@
     j = lax.axis_index("img")
     core = i & 1
     row = i >> 1
+    x, y, z = row & 3, j & 3, 2 * (j >> 2) + (row >> 2)
     sibling = (i + 1 - 2 * core, j)
     own = (own_0, own_1, own_2, own_3)
     sib = (sib_0, sib_1, sib_2, sib_3)
@@ -212,29 +211,6 @@
         c.wait()
     ramp_tiles(ramp_hi, ramp_fine)
 
-    def source_angle(stage, q, a):
-        chip = (row - (2 * (stage >> 1) + q)) & 7
-        side = core ^ (stage & 1)
-        return 4 * chip + 2 * side + a
-
-    pixel = lax.broadcasted_iota(jnp.int32, (1, TILE * TILE), 1)
-    px = (pixel & (TILE - 1)).astype(jnp.float32) * 0.0625
-    py = (pixel >> 5).astype(jnp.float32) * 0.0625
-    slot = lax.broadcasted_iota(jnp.int32, (128, TILE * TILE), 0).astype(jnp.float32)
-
-    @pl.loop(0, 8)
-    def _(stage):
-        for q in range(2):
-            for a in range(2):
-                offset, u, v, low = angle_data(offsets, steps, source_angle(stage, q, a))
-                first = ((offset + low * (TILE - 1)) & 15) - low * (TILE - 1)
-                where = (
-                    first.astype(jnp.float32) * 0.0625 + u.astype(jnp.float32) * px + v.astype(jnp.float32) * py
-                )
-                weights[stage, pl.ds(256 * q + 128 * a, 128)] = jnp.maximum(
-                    1.0 - jnp.abs(slot - where), 0.0
-                ).astype(jnp.bfloat16)
-
     for c in row_copies:
         c.wait_recv()
     filter_rows(rows, filt_acc, filt, ramp_hi, ramp_fine)
@@ -250,42 +226,61 @@
         rolled = [pltpu.roll(blocks[n], back, 1) for n in range(4)]
         return [jnp.where(lane < 128 - shift, rolled[n], rolled[n + 1]) for n in range(3)]
 
-    def window_copy(group, k, part, q):
-        r = (row + group) & 7
-        c = (j + k) & 7
+    def partner(p, dx, dy):
+        xt, yt, zt = (x + dx) & 3, (y + dy) & 3, (z + dx + p) & 3
+        return 4 * (zt & 1) + xt, 4 * (zt >> 1) + yt
+
+    def window_copy(p, dx, dy):
+        r, c = partner(p, dx, dy)
         return pltpu.make_async_remote_copy(
-            src_ref=packed.at[group, k],
-            dst_ref=part.at[q, j],
-            send_sem=win_send.at[group],
-            recv_sem=win_recv.at[group],
+            src_ref=packed.at[p, 4 * dx + dy],
+            dst_ref=own[p].at[4 * dx + y],
+            send_sem=win_send.at[p],
+            recv_sem=win_recv.at[p],
             device_id=(2 * r + core, c),
             device_id_type=MESH,
         )
 
-    def group_copy(group, part, q, count):
+    def stage_copy(p):
+        count = 15 if p == 0 else 16
         return pltpu.make_async_remote_copy(
-            src_ref=packed.at[group, pl.ds(IMGD - count, count)],
-            dst_ref=part.at[q, pl.ds(0, count)],
-            send_sem=win_send.at[group],
-            recv_sem=win_recv.at[group],
+            src_ref=packed.at[p, pl.ds(16 - count, count)],
+            dst_ref=own[p].at[pl.ds(0, count)],
+            send_sem=win_send.at[p],
+            recv_sem=win_recv.at[p],
             device_id=sibling,
             device_id_type=MESH,
         )
 
-    for n, block in enumerate(pack(row, j)):
-        own_0[0, j, n] = block
-    for group in range(8):
-        r = (row + group) & 7
-        ks = range(1 if group == 0 else 0, IMGD)
-        for half in (ks[: len(ks) // 2], ks[len(ks) // 2 :]):
-            for k in half:
-                for n, block in enumerate(pack(r, (j + k) & 7)):
-                    packed[group, k, n] = block
-            for k in half:
-                window_copy(group, k, own[group // 2], group % 2).start()
-
-    def group_waits(p):
-        return [group_copy(2 * p + q, own[p], q, 7 if 2 * p + q == 0 else 8) for q in range(2)]
+    for p in range(4):
+        for dy in range(4):
+            for dx in range(4):
+                mine = p == 0 and dx == 0 and dy == 0
+                for n, block in enumerate(pack(*partner(p, dx, dy))):
+                    if mine:
+                        own_0[y, n] = block
+                    else:
+                        packed[p, 4 * dx + dy, n] = block
+            for dx in range(4):
+                if p + dx + dy > 0:
+                    window_copy(p, dx, dy).start()
+
+    def source_angle(p, side, dx):
+        xs, zs = (x - dx) & 3, (z - dx - p) & 3
+        return 4 * (4 * (zs & 1) + xs) + 2 * (core ^ side) + (zs >> 1)
+
+    pixel = lax.broadcasted_iota(jnp.int32, (1, TILE * TILE), 1)
+    px = (pixel & (TILE - 1)).astype(jnp.float32) * 0.0625
+    py = (pixel >> 5).astype(jnp.float32) * 0.0625
+    slot = lax.broadcasted_iota(jnp.int32, (128, TILE * TILE), 0).astype(jnp.float32)
+
+    @pl.loop(0, 8)
+    def _(stage):
+        for dx in range(4):
+            offset, u, v, low = angle_data(offsets, steps, source_angle(stage >> 1, stage & 1, dx))
+            first = ((offset + low * (TILE - 1)) & 15) - low * (TILE - 1)
+            where = first.astype(jnp.float32) * 0.0625 + u.astype(jnp.float32) * px + v.astype(jnp.float32) * py
+            weights[stage, pl.ds(128 * dx, 128)] = jnp.maximum(1.0 - jnp.abs(slot - where), 0.0).astype(jnp.bfloat16)
 
     def share_copy(p):
         return pltpu.make_async_remote_copy(
@@ -298,48 +293,42 @@
         )
 
     def arrive(p):
-        for c in group_waits(p):
-            c.wait_recv()
+        stage_copy(p).wait_recv()
         share_copy(p).start()
 
     def prepare(stage, n):
-        p = stage // 2
-        place_lhs(
-            (own if stage % 2 == 0 else sib)[p],
-            (lhs_0, lhs_1)[n % 2],
-            offsets,
-            steps,
-            lambda q, a: source_angle(stage, q, a),
-        )
+        p, side = stage // 2, stage % 2
+        place_lhs((own, sib)[side][p], (lhs_0, lhs_1)[n % 2], offsets, steps, lambda dx: source_angle(p, side, dx))
 
     order = (0, 2, 1, 4, 3, 6, 5, 7)
     arrive(0)
     prepare(0, 0)
-    for n, stage in enumerate(order):
-        if n + 1 < 8:
-            after = order[n + 1]
-            if after in (2, 4, 6):
-                arrive(after // 2)
-            if after % 2 == 1:
-                share_copy(after // 2).wait_recv()
-            prepare(after, n + 1)
+    for n, stage in enumerate(order[:-1]):
+        after = order[n + 1]
+        if after in (2, 4, 6):
+            arrive(after // 2)
+        if after % 2 == 1:
+            share_copy(after // 2).wait_recv()
+        prepare(after, n + 1)
         total = jnp.dot((lhs_0, lhs_1)[n % 2][...], weights[stage], preferred_element_type=jnp.float32)
         if n == 0:
             acc[...] = total
         else:
             acc[...] += total
-    store_picture(acc, out)
+    for part in range(4):
+        at = pl.ds(256 * part, 256)
+        total = acc[:, at] + jnp.dot(lhs_1[...], weights[7, :, at], preferred_element_type=jnp.float32)
+        store_rows(total, out, 8 * part)
     for c in row_copies:
         c.wait_send()
     for p in range(4):
         share_copy(p).wait_send()
-        for c in group_waits(p):
-            c.wait_send()
+        stage_copy(p).wait_send()
 
 
 def shards(sinogram, offsets, steps):
     vmem = pl.BlockSpec(memory_space=pltpu.VMEM)
-    hbm = pl.BlockSpec(memory_space=pl.ANY)
+    hbm = pl.BlockSpec(memory_space=pltpu.HBM)
     window = (3, GROUP, 128)
     return pl.pallas_call(
         whole_kernel,
@@ -350,8 +339,8 @@
             pltpu.SMEM((ANGLES,), jnp.int32),
             pltpu.SMEM((2, ANGLES), jnp.int32),
             pltpu.VMEM((IMGD, GROUP, BINS // IMGD), jnp.bfloat16),
-            pltpu.VMEM((8, IMGD, *window), jnp.bfloat16),
-            *([pltpu.VMEM((2, IMGD, *window), jnp.bfloat16)] * 8),
+            pltpu.VMEM((4, 16, *window), jnp.bfloat16),
+            *([pltpu.VMEM((16, *window), jnp.bfloat16)] * 8),
             pltpu.VMEM((64, 128, 128), jnp.bfloat16),
             pltpu.VMEM((2, 7, 128, 128), jnp.bfloat16),
             pltpu.VMEM((16, GROUP, 256), jnp.float32),
@@ -363,8 +352,8 @@
             pltpu.SemaphoreType.DMA((3,)),
             pltpu.SemaphoreType.DMA((IMGD,)),
             pltpu.SemaphoreType.DMA((IMGD,)),
-            pltpu.SemaphoreType.DMA((8,)),
-            pltpu.SemaphoreType.DMA((8,)),
+            pltpu.SemaphoreType.DMA((4,)),
+            pltpu.SemaphoreType.DMA((4,)),
             pltpu.SemaphoreType.DMA((4,)),
             pltpu.SemaphoreType.DMA((4,)),
         ],

time: 38.5 us -> 37 us (0.961)
  Pallas kernels: 35.6 us -> 34.1 us
    pallas_call x1, Pallas kernels: 35.6 us -> 34.1 us  [shards(): pl.pallas_call(whole_kernel, out_shape=jax.ShapeDtypeStruct((ROWS, SLICES...]
where the time goes in v4:
time: 37 us; the launch traced here: 36.7 us
  Pallas kernels  34.1 us (92%)
  local copies, waits for them, and re-layouts  2.56 us (7%)
    pallas_call x1, Pallas kernels, shards(): pl.pallas_call(whole_kernel, out_shape=jax.ShapeDtypeStruct((ROWS, SLICES...  34.1 us
    unnamed x7, local copies, waits for them, and re-layouts  2.56 us

profile of v4, /device:TPU:1, one launch (start us, length us, event | category | flops | bytes accessed | tf_op | source)
XLA Modules:
  0.0 36.7 jit_solution(14827483563542232510)
XLA Ops:
  0.0 0.0 copy-start.1
  0.0 0.0 copy-start.2
  0.0 0.7 %copy-done.1 = s32[32,2]{0,1:T(2,128)S(1)} copy-done((s32[32,2]{0,1:T(2,128)S(1)}, s32[32,2]{0,1:T(2,128)}, u32[]{:S(2)}) %copy-start.1) | copy-done | bytes 280
  0.7 0.0 copy-done.2
  0.7 0.0 copy-start
  0.7 0.9 %copy-done = bf16[2,64,512]{2,1,0:T(8,128)(2,1)S(1)} copy-done((bf16[2,64,512]{2,1,0:T(8,128)(2,1)S(1)}, bf16[2,64,512]{2,1,0:T(8,128)(2,1)}, u32[]{:S(2)}) %copy-start) | copy-done | bytes 131096
  1.6 34.1 %back_projection.1 = bf16[64,64,128]{2,1,0:T(8,128)(2,1)S(1)} custom-call(s32[32]{0:T(128)S(1)} %copy-done.2, s32[2,32]{1,0:T(2,128)S(1)} %bitcast.3, bf16[8,16,512]{2,1,0:T(8,128)(2,1)S(1)} %bitcast.2), custom_call_target="tpu_custom_call" | custom-call | tf_op jit(solution)/shard_map/back_projection/pallas_call | solution.py:333
  35.7 1.0 %copy.5 = bf16[64,64,128]{2,1,0:T(8,128)(2,1)} copy(bf16[64,64,128]{2,1,0:T(8,128)(2,1)S(1)} %back_projection.1) | data formatting | bytes 2097152
Async XLA Ops:
  0.0 0.7 %copy-start.1 = (s32[32,2]{0,1:T(2,128)S(1)}, s32[32,2]{0,1:T(2,128)}, u32[]{:S(2)}) copy-start(s32[32,2]{0,1:T(2,128)} %param.5) | copy-start | bytes 772
  0.0 0.7 %copy-start.2 = (s32[32]{0:T(128)S(1)}, s32[32]{0:T(128)}, u32[]{:S(2)}) copy-start(s32[32]{0:T(128)} %offsets_in.1) | copy-start | bytes 388
  0.7 0.9 %copy-start = (bf16[2,64,512]{2,1,0:T(8,128)(2,1)S(1)}, bf16[2,64,512]{2,1,0:T(8,128)(2,1)}, u32[]{:S(2)}) copy-start(bf16[2,64,512]{2,1,0:T(8,128)(2,1)} %param.3) | copy-start | bytes 393220

commit v5 on v4

--- a/solution.py
+++ b/solution.py
@@ -89,7 +89,7 @@
     return (offset + u * (COLS * img) + v * (2 * ROWS * chip_row) + low * 127) >> 4
 
 
-def place_lhs(part, lhs, offsets, steps, angle_of):
+def place_lhs(windows, p, lhs, offsets, steps, angle_of):
     i = lax.axis_index("ang")
     j = lax.axis_index("img")
     lane = lax.broadcasted_iota(jnp.int32, (1, 128), 1)
@@ -97,18 +97,16 @@
         offset, u, v, low = angle_data(offsets, steps, angle_of(dx))
         ws = window_start(offset, u, v, low, i >> 1, j)
         base = offset + u * (COLS * j) + v * (ROWS * i) + low * (TILE - 1)
+        blocks = [windows[p, pl.ds(4 * dx, 4), n].reshape(SLICES, 128) for n in range(3)]
         for tile in range(TILES):
             ty, tx = tile // 4, tile % 4
             begin = ((base + u * (TILE * tx) + v * (TILE * ty)) >> 4) - ws
-            block = begin >> 7
-            shift = begin & 127
-            back = (128 - shift) & 127
-            after = jnp.minimum(block + 1, 2)
-            left = part[pl.ds(4 * dx, 4), block].reshape(SLICES, 128)
-            right = part[pl.ds(4 * dx, 4), after].reshape(SLICES, 128)
+            back = (128 - (begin & 127)) & 127
+            left = jnp.where(begin < 128, blocks[0], jnp.where(begin < 256, blocks[1], blocks[2]))
+            right = jnp.where(begin < 128, blocks[1], blocks[2])
             left = pltpu.roll(left, back, 1)
             right = pltpu.roll(right, back, 1)
-            band = jnp.where(lane < 128 - shift, left, right)
+            band = jnp.where(lane < 128 - (begin & 127), left, right)
             lhs[pl.ds(tile * SLICES, SLICES), pl.ds(128 * dx, 128)] = band
 
 
@@ -145,14 +143,8 @@
     steps,
     rows,
     packed,
-    own_0,
-    own_1,
-    own_2,
-    own_3,
-    sib_0,
-    sib_1,
-    sib_2,
-    sib_3,
+    own,
+    sib,
     ramp_hi,
     ramp_fine,
     filt_acc,
@@ -175,8 +167,6 @@
     row = i >> 1
     x, y, z = row & 3, j & 3, 2 * (j >> 2) + (row >> 2)
     sibling = (i + 1 - 2 * core, j)
-    own = (own_0, own_1, own_2, own_3)
-    sib = (sib_0, sib_1, sib_2, sib_3)
 
     barrier = pltpu.get_barrier_semaphore()
     for k in range(1, IMGD):
@@ -234,36 +224,39 @@
         r, c = partner(p, dx, dy)
         return pltpu.make_async_remote_copy(
             src_ref=packed.at[p, 4 * dx + dy],
-            dst_ref=own[p].at[4 * dx + y],
+            dst_ref=own.at[p, 4 * dx + y],
             send_sem=win_send.at[p],
             recv_sem=win_recv.at[p],
             device_id=(2 * r + core, c),
             device_id_type=MESH,
         )
 
-    def stage_copy(p):
-        count = 15 if p == 0 else 16
+    def stage_copy(p, count=16):
         return pltpu.make_async_remote_copy(
             src_ref=packed.at[p, pl.ds(16 - count, count)],
-            dst_ref=own[p].at[pl.ds(0, count)],
+            dst_ref=own.at[p, pl.ds(0, count)],
             send_sem=win_send.at[p],
             recv_sem=win_recv.at[p],
             device_id=sibling,
             device_id_type=MESH,
         )
 
-    for p in range(4):
-        for dy in range(4):
-            for dx in range(4):
-                mine = p == 0 and dx == 0 and dy == 0
-                for n, block in enumerate(pack(*partner(p, dx, dy))):
-                    if mine:
-                        own_0[y, n] = block
-                    else:
-                        packed[p, 4 * dx + dy, n] = block
-            for dx in range(4):
-                if p + dx + dy > 0:
-                    window_copy(p, dx, dy).start()
+    def pack_row(p, dy):
+        for dx in range(4):
+            for n, block in enumerate(pack(*partner(p, dx, dy))):
+                packed[p, 4 * dx + dy, n] = block
+
+    pack_row(0, 0)
+    for dx in range(1, 4):
+        window_copy(0, dx, 0).start()
+    own[0, y] = packed[0, 0]
+
+    @pl.loop(1, 16)
+    def _(t):
+        p, dy = t >> 2, t & 3
+        pack_row(p, dy)
+        for dx in range(4):
+            window_copy(p, dx, dy).start()
 
     def source_angle(p, side, dx):
         xs, zs = (x - dx) & 3, (z - dx - p) & 3
@@ -284,46 +277,50 @@
 
     def share_copy(p):
         return pltpu.make_async_remote_copy(
-            src_ref=own[p],
-            dst_ref=sib[p],
+            src_ref=own.at[p],
+            dst_ref=sib.at[p],
             send_sem=sib_send.at[p],
             recv_sem=sib_recv.at[p],
             device_id=sibling,
             device_id_type=MESH,
         )
 
-    def arrive(p):
+    def prepare(p, side, lhs):
+        place_lhs((own, sib)[side], p, lhs, offsets, steps, lambda dx: source_angle(p, side, dx))
+
+    def multiply(lhs, stage):
+        acc[...] += jnp.dot(lhs[...], weights[stage], preferred_element_type=jnp.float32)
+
+    acc[...] = jnp.zeros_like(acc)
+    stage_copy(0, 15).wait_recv()
+    share_copy(0).start()
+    prepare(0, 0, lhs_0)
+
+    @pl.loop(1, 4)
+    def _(p):
         stage_copy(p).wait_recv()
         share_copy(p).start()
-
-    def prepare(stage, n):
-        p, side = stage // 2, stage % 2
-        place_lhs((own, sib)[side][p], (lhs_0, lhs_1)[n % 2], offsets, steps, lambda dx: source_angle(p, side, dx))
-
-    order = (0, 2, 1, 4, 3, 6, 5, 7)
-    arrive(0)
-    prepare(0, 0)
-    for n, stage in enumerate(order[:-1]):
-        after = order[n + 1]
-        if after in (2, 4, 6):
-            arrive(after // 2)
-        if after % 2 == 1:
-            share_copy(after // 2).wait_recv()
-        prepare(after, n + 1)
-        total = jnp.dot((lhs_0, lhs_1)[n % 2][...], weights[stage], preferred_element_type=jnp.float32)
-        if n == 0:
-            acc[...] = total
-        else:
-            acc[...] += total
-    for part in range(4):
-        at = pl.ds(256 * part, 256)
+        prepare(p, 0, lhs_1)
+        multiply(lhs_0, jnp.maximum(2 * p - 3, 0))
+        share_copy(p - 1).wait_recv()
+        prepare(p - 1, 1, lhs_0)
+        multiply(lhs_1, 2 * p)
+
+    share_copy(3).wait_recv()
+    prepare(3, 1, lhs_1)
+    multiply(lhs_0, 5)
+
+    @pl.loop(0, 4)
+    def _(part):
+        at = pl.ds(pl.multiple_of(256 * part, 256), 256)
         total = acc[:, at] + jnp.dot(lhs_1[...], weights[7, :, at], preferred_element_type=jnp.float32)
         store_rows(total, out, 8 * part)
+
     for c in row_copies:
         c.wait_send()
     for p in range(4):
         share_copy(p).wait_send()
-        stage_copy(p).wait_send()
+        stage_copy(p, 15 if p == 0 else 16).wait_send()
 
 
 def shards(sinogram, offsets, steps):
@@ -340,7 +337,7 @@
             pltpu.SMEM((2, ANGLES), jnp.int32),
             pltpu.VMEM((IMGD, GROUP, BINS // IMGD), jnp.bfloat16),
             pltpu.VMEM((4, 16, *window), jnp.bfloat16),
-            *([pltpu.VMEM((16, *window), jnp.bfloat16)] * 8),
+            *([pltpu.VMEM((4, 16, *window), jnp.bfloat16)] * 2),
             pltpu.VMEM((64, 128, 128), jnp.bfloat16),
             pltpu.VMEM((2, 7, 128, 128), jnp.bfloat16),
             pltpu.VMEM((16, GROUP, 256), jnp.float32),
@@ -359,7 +356,11 @@
         ],
         compiler_params=pltpu.CompilerParams(collective_id=0, has_side_effects=True, vmem_limit_bytes=LIMIT),
         name="back_projection",
-    )(offsets, steps.T, sinogram.reshape(IMGD, GROUP, BINS // IMGD))
+    )(
+        pltpu.with_memory_space_constraint(offsets, pltpu.HBM),
+        pltpu.with_memory_space_constraint(steps.T, pltpu.HBM),
+        pltpu.with_memory_space_constraint(sinogram.reshape(IMGD, GROUP, BINS // IMGD), pltpu.HBM),
+    )
 
 
 def solution(mesh):

time: 37 us -> 32.8 us (0.89)
  Pallas kernels: 34.1 us -> 31.7 us
  local copies, waits for them, and re-layouts: 2.56 us -> 0.97 us
    pallas_call x1, Pallas kernels: 34.1 us -> 31.7 us  [shards(): pl.pallas_call(whole_kernel, out_shape=jax.ShapeDtypeStruct((ROWS, SLICES...]
    unnamed x7 -> x1, local copies, waits for them, and re-layouts: 2.56 us -> 0.97 us
where the time goes in v5:
time: 32.8 us; the launch traced here: 32.7 us
  Pallas kernels  31.7 us (97%)
  local copies, waits for them, and re-layouts  0.97 us (3%)
    pallas_call x1, Pallas kernels, shards(): pl.pallas_call(whole_kernel, out_shape=jax.ShapeDtypeStruct((ROWS, SLICES...  31.7 us
    unnamed x1, local copies, waits for them, and re-layouts  0.97 us

profile of v5, /device:TPU:1, one launch (start us, length us, event | category | flops | bytes accessed | tf_op | source)
XLA Modules:
  0.0 32.7 jit_solution(13032472154700619206)
XLA Ops:
  0.0 31.7 %back_projection.1 = bf16[64,64,128]{2,1,0:T(8,128)(2,1)S(1)} custom-call(s32[32]{0:T(128)} %offsets_in.1, s32[2,32]{1,0:T(2,128)} %bitcast.3, bf16[8,16,512]{2,1,0:T(8,128)(2,1)} %bitcast.2), custom_call_target="tpu_custom_call" | custom-call | tf_op jit(solution)/shard_map/back_projection/pallas_call | solution.py:330
  31.7 1.0 %copy.5 = bf16[64,64,128]{2,1,0:T(8,128)(2,1)} copy(bf16[64,64,128]{2,1,0:T(8,128)(2,1)S(1)} %back_projection.1) | data formatting | bytes 2097152

commit v6 on v5

--- a/solution.py
+++ b/solution.py
@@ -306,9 +306,9 @@
         prepare(p - 1, 1, lhs_0)
         multiply(lhs_1, 2 * p)
 
+    multiply(lhs_0, 5)
     share_copy(3).wait_recv()
     prepare(3, 1, lhs_1)
-    multiply(lhs_0, 5)
 
     @pl.loop(0, 4)
     def _(part):

time: 32.8 us -> 32.4 us (0.988)
    pallas_call x1, Pallas kernels: 31.7 us -> 31.4 us  [shards(): pl.pallas_call(whole_kernel, out_shape=jax.ShapeDtypeStruct((ROWS, SLICES...]
where the time goes in v6:
time: 32.4 us; the launch traced here: 32.3 us
  Pallas kernels  31.4 us (97%)
  local copies, waits for them, and re-layouts  0.97 us (3%)
    pallas_call x1, Pallas kernels, shards(): pl.pallas_call(whole_kernel, out_shape=jax.ShapeDtypeStruct((ROWS, SLICES...  31.4 us
    unnamed x1, local copies, waits for them, and re-layouts  0.97 us

profile of v6, /device:TPU:1, one launch (start us, length us, event | category | flops | bytes accessed | tf_op | source)
XLA Modules:
  0.0 32.3 jit_solution(13092517172117621434)
XLA Ops:
  0.0 31.4 %back_projection.1 = bf16[64,64,128]{2,1,0:T(8,128)(2,1)S(1)} custom-call(s32[32]{0:T(128)} %offsets_in.1, s32[2,32]{1,0:T(2,128)} %bitcast.3, bf16[8,16,512]{2,1,0:T(8,128)(2,1)} %bitcast.2), custom_call_target="tpu_custom_call" | custom-call | tf_op jit(solution)/shard_map/back_projection/pallas_call | solution.py:330
  31.4 1.0 %copy.5 = bf16[64,64,128]{2,1,0:T(8,128)(2,1)} copy(bf16[64,64,128]{2,1,0:T(8,128)(2,1)S(1)} %back_projection.1) | data formatting | bytes 2097152

commit v7 on v6

--- a/solution.py
+++ b/solution.py
@@ -310,11 +310,11 @@
     share_copy(3).wait_recv()
     prepare(3, 1, lhs_1)
 
-    @pl.loop(0, 4)
+    @pl.loop(0, 2)
     def _(part):
-        at = pl.ds(pl.multiple_of(256 * part, 256), 256)
+        at = pl.ds(pl.multiple_of(512 * part, 512), 512)
         total = acc[:, at] + jnp.dot(lhs_1[...], weights[7, :, at], preferred_element_type=jnp.float32)
-        store_rows(total, out, 8 * part)
+        store_rows(total, out, 16 * part)
 
     for c in row_copies:
         c.wait_send()

time: 32.4 us -> 31.9 us (0.985)
  Pallas kernels: 31.4 us -> 30.9 us
    pallas_call x1, Pallas kernels: 31.4 us -> 30.9 us  [shards(): pl.pallas_call(whole_kernel, out_shape=jax.ShapeDtypeStruct((ROWS, SLICES...]
where the time goes in v7:
time: 31.9 us; the launch traced here: 31.8 us
  Pallas kernels  30.9 us (97%)
  local copies, waits for them, and re-layouts  0.97 us (3%)
    pallas_call x1, Pallas kernels, shards(): pl.pallas_call(whole_kernel, out_shape=jax.ShapeDtypeStruct((ROWS, SLICES...  30.9 us
    unnamed x1, local copies, waits for them, and re-layouts  0.97 us

profile of v7, /device:TPU:1, one launch (start us, length us, event | category | flops | bytes accessed | tf_op | source)
XLA Modules:
  0.0 31.8 jit_solution(6368961143610236689)
XLA Ops:
  0.0 30.9 %back_projection.1 = bf16[64,64,128]{2,1,0:T(8,128)(2,1)S(1)} custom-call(s32[32]{0:T(128)} %offsets_in.1, s32[2,32]{1,0:T(2,128)} %bitcast.3, bf16[8,16,512]{2,1,0:T(8,128)(2,1)} %bitcast.2), custom_call_target="tpu_custom_call" | custom-call | tf_op jit(solution)/shard_map/back_projection/pallas_call | solution.py:330
  30.9 1.0 %copy.5 = bf16[64,64,128]{2,1,0:T(8,128)(2,1)} copy(bf16[64,64,128]{2,1,0:T(8,128)(2,1)S(1)} %back_projection.1) | data formatting | bytes 2097152

commit v8 on v7

--- a/solution.py
+++ b/solution.py
@@ -310,9 +310,8 @@
     share_copy(3).wait_recv()
     prepare(3, 1, lhs_1)
 
-    @pl.loop(0, 2)
-    def _(part):
-        at = pl.ds(pl.multiple_of(512 * part, 512), 512)
+    for part in range(2):
+        at = pl.ds(512 * part, 512)
         total = acc[:, at] + jnp.dot(lhs_1[...], weights[7, :, at], preferred_element_type=jnp.float32)
         store_rows(total, out, 16 * part)
 

time: 31.9 us -> 31.4 us (0.984)
  Pallas kernels: 30.9 us -> 30.3 us
    pallas_call x1, Pallas kernels: 30.9 us -> 30.3 us  [shards(): pl.pallas_call(whole_kernel, out_shape=jax.ShapeDtypeStruct((ROWS, SLICES...]
where the time goes in v8:
time: 31.4 us; the launch traced here: 31.3 us
  Pallas kernels  30.3 us (96%)
  local copies, waits for them, and re-layouts  0.97 us (3%)
    pallas_call x1, Pallas kernels, shards(): pl.pallas_call(whole_kernel, out_shape=jax.ShapeDtypeStruct((ROWS, SLICES...  30.3 us
    unnamed x1, local copies, waits for them, and re-layouts  0.97 us

profile of v8, /device:TPU:1, one launch (start us, length us, event | category | flops | bytes accessed | tf_op | source)
XLA Modules:
  0.0 31.3 jit_solution(11402493798962787011)
XLA Ops:
  0.0 30.3 %back_projection.1 = bf16[64,64,128]{2,1,0:T(8,128)(2,1)S(1)} custom-call(s32[32]{0:T(128)} %offsets_in.1, s32[2,32]{1,0:T(2,128)} %bitcast.3, bf16[8,16,512]{2,1,0:T(8,128)(2,1)} %bitcast.2), custom_call_target="tpu_custom_call" | custom-call | tf_op jit(solution)/shard_map/back_projection/pallas_call | solution.py:329
  30.3 1.0 %copy.5 = bf16[64,64,128]{2,1,0:T(8,128)(2,1)} copy(bf16[64,64,128]{2,1,0:T(8,128)(2,1)S(1)} %back_projection.1) | data formatting | bytes 2097152
